TPU v7x, 32 devices: a whole 2x2x4 slice. The times are simulated.
32 devices in a mesh: alpha: 8 (over z, x), beta: 4 (over y, core).
Axes of the slice: x: 2, y: 2, z: 4, core: 2. Of those that a mesh axis runs over, the one named last changes fastest.
Arguments:
- coeffs: bfloat16 [2048, 4096], P('alpha', 'beta'), may hold values from -6 to 6
- a_blocks: bfloat16 [2, 2048, 11, 128], P(None, 'alpha'), may hold values from -0.15625 to 0.15625
- a_list: int32 [2, 16, 11], replicated, may hold values from 0 to 15, as said below
- a_count: int32 [2, 16], replicated, may hold values from 4 to 11, as said below
- b_blocks: bfloat16 [2, 4096, 11, 128], P(None, 'beta'), may hold values from -0.15625 to 0.15625
- b_list: int32 [2, 32, 11], replicated, may hold values from 0 to 31, as said below
- b_count: int32 [2, 32], replicated, may hold values from 4 to 11, as said below
Outputs:
- sigma: float32 [2048, 4096], P('alpha', 'beta')
Inputs may be any that keep to these rules, and one draw needn't show every extreme that they name: `a_list`: every entry, valid slot or not, is an alpha block number. For each index r of alpha and each index o of alpha, the entries of all operators in the rows of blocks r * 2 to r * 2 + 1 that lie in blocks o * 2 to o * 2 + 1 name at most 1 distinct blocks, and some pair names exactly 1. `b_list`: the same with beta, 8 and 2. `a_count`: some row has all 11 slots valid. `b_count`: some row has all 11 slots valid.
All inputs are finite; a program needn't handle non-finite values.
Results may differ from a plain program's by a relative error of at most 0.0029.
Values may be sent and summed in bfloat16 or wider, within the bound.
A program may use at most 128 MiB of HBM per device.

v0:
```python
import functools

import jax
import jax.numpy as jnp
from jax import lax
from jax.experimental import pallas as pl
from jax.experimental.pallas import tpu as pltpu
from jax.sharding import PartitionSpec as P

FROM_A = 1
FROM_B = 2
PAIR = 2
VMEM_LIMIT = 60 * 1024 * 1024
MESH = pl.DeviceIdType.MESH


def pick_kernel(geometry, a_lists, b_lists, c_ref, picks_ref, small):
    na, nb, ops, slots, blk, row_blocks, col_blocks = geometry
    a = lax.axis_index("alpha")
    c = lax.axis_index("beta")
    lists = b_lists[...]
    lane = lax.broadcasted_iota(jnp.int32, (1, nb * col_blocks), 1)

    def extremes(receiver, owner):
        local = lists - owner * col_blocks
        hit = (local >= 0) & (local < col_blocks)
        rows_here = (lane >= receiver * col_blocks) & (lane < (receiver + 1) * col_blocks)
        low = jnp.min(jnp.min(jnp.where(hit, local, col_blocks), axis=0), axis=0, keepdims=True)
        high = jnp.max(jnp.max(jnp.where(hit, local, 0), axis=0), axis=0, keepdims=True)
        low = jnp.min(jnp.where(rows_here, low, col_blocks))
        high = jnp.max(jnp.where(rows_here, high, 0))
        return jnp.where(low < col_blocks, low, 0), high

    for j in range(nb):
        for u, block in enumerate(extremes(c ^ j, c)):
            picks_ref[j, :, u * blk:(u + 1) * blk] = c_ref[:, pl.ds(pl.multiple_of(block * blk, blk), blk)]
    for owner in range(nb):
        small[2 * na + owner] = extremes(c, owner)[0]
    for n in range(2 * na):
        small[n] = 0
    for side in range(2):
        receiver = a ^ side
        for k in range(ops):
            for i in range(row_blocks):
                for s in range(slots):
                    entry = a_lists[s, k, receiver * row_blocks + i]
                    owner = lax.div(entry, row_blocks)
                    small[side * na + owner] = entry - owner * row_blocks


def sigma_kernel(geometry, small, a_lists, a_counts, b_lists, b_counts, picks, a_hbm, b_hbm, out_ref, abuf, bbuf, column, across, chosen, adense, bdense, acc,
                 local_sem, beta_send, beta_recv, column_recv, up_send, down_send, across_send, across_recv):
    na, nb, ops, slots, blk, row_blocks, col_blocks = geometry
    levels = na // PAIR
    rows = row_blocks * blk
    wide = FROM_B * blk
    a = lax.axis_index("alpha")
    c = lax.axis_index("beta")
    z = a // PAIR
    x = a % PAIR
    partner = a + 1 - 2 * x
    at_low = 2 * na

    def one_hot(value, place):
        gap = value - place
        return (1 - jnp.minimum(jnp.maximum(gap, -gap), 1)).astype(jnp.float32)

    def at_most(slot, count):
        return jnp.minimum(jnp.maximum(count - slot, 0), 1)

    copy_a = pltpu.make_async_copy(a_hbm, abuf, local_sem.at[0])
    copy_b = pltpu.make_async_copy(b_hbm, bbuf, local_sem.at[1])
    copy_a.start()
    copy_b.start()

    column[z, 0] = picks[0]

    barrier = pltpu.get_barrier_semaphore()
    for j in range(1, nb):
        pl.semaphore_signal(barrier, inc=1, device_id={"beta": c ^ j}, device_id_type=MESH)
    pl.semaphore_signal(barrier, inc=1, device_id={"alpha": partner}, device_id_type=MESH)

    @pl.when(z < levels - 1)
    def _():
        pl.semaphore_signal(barrier, inc=1, device_id={"alpha": a + PAIR}, device_id_type=MESH)

    @pl.when(z > 0)
    def _():
        pl.semaphore_signal(barrier, inc=1, device_id={"alpha": a - PAIR}, device_id_type=MESH)

    neighbours = nb + jnp.where(z < levels - 1, 1, 0) + jnp.where(z > 0, 1, 0)
    pl.semaphore_wait(barrier, neighbours)

    def beta_copy(j):
        return pltpu.make_async_remote_copy(
            src_ref=picks.at[j], dst_ref=column.at[z, j], send_sem=beta_send.at[j - 1], recv_sem=beta_recv.at[j - 1],
            device_id={"beta": c ^ j}, device_id_type=MESH)

    def up_copy(lev, j):
        return pltpu.make_async_remote_copy(
            src_ref=column.at[lev, j], dst_ref=column.at[lev, j], send_sem=up_send.at[lev, j], recv_sem=column_recv.at[lev, j],
            device_id={"alpha": a + PAIR}, device_id_type=MESH)

    def down_copy(lev, j):
        return pltpu.make_async_remote_copy(
            src_ref=column.at[lev, j], dst_ref=column.at[lev, j], send_sem=down_send.at[lev, j], recv_sem=column_recv.at[lev, j],
            device_id={"alpha": a - PAIR}, device_id_type=MESH)

    def across_copy(lev, j):
        return pltpu.make_async_remote_copy(
            src_ref=chosen.at[lev, j], dst_ref=across.at[lev, j], send_sem=across_send.at[lev, j], recv_sem=across_recv.at[lev, j],
            device_id={"alpha": partner}, device_id_type=MESH)

    for j in range(1, nb):
        beta_copy(j).start()

    acc[...] = jnp.zeros_like(acc)
    out_ref[...] = jnp.zeros_like(out_ref)

    def build_a():
        copy_a.wait()

        def per_owner(o, carry):
            for k in range(ops):
                for i in range(row_blocks):
                    total = jnp.zeros((blk, blk), jnp.float32)
                    for s in range(slots):
                        entry = a_lists[s, k, a * row_blocks + i]
                        valid = at_most(s, a_counts[k, a * row_blocks + i])
                        weight = one_hot(lax.div(entry, row_blocks), o) * valid.astype(jnp.float32)
                        total += abuf[k, s, i * blk:(i + 1) * blk, :].astype(jnp.float32) * weight
                    high = total.astype(jnp.bfloat16)
                    low = (total - high.astype(jnp.float32)).astype(jnp.bfloat16)
                    at = k * rows + i * blk
                    adense[o, 0, at:at + blk, :] = high
                    adense[o, 1, at:at + blk, :] = low
            return carry

        lax.fori_loop(0, na, per_owner, 0)

    def build_b(piece):
        k = piece // col_blocks
        r = piece % col_blocks
        here = pl.ds(pl.multiple_of(r * blk, blk), blk)
        codes = []
        for s in range(slots):
            entry = b_lists[s, k, c * col_blocks + r]
            owner = lax.div(entry, col_blocks)
            gap = entry - owner * col_blocks - small[at_low + owner]
            place = (owner ^ c) * FROM_B + jnp.minimum(jnp.maximum(gap, -gap), 1)
            valid = at_most(s, b_counts[k, c * col_blocks + r])
            codes.append((place + 1) * valid - 1)

        def per_chunk(j, carry):
            for u in range(FROM_B):
                total = jnp.zeros((blk, blk), jnp.float32)
                for s in range(slots):
                    weight = one_hot(codes[s], j * FROM_B + u)
                    total += bbuf[k, s, here, :].astype(jnp.float32) * weight
                high = total.astype(jnp.bfloat16)
                low = (total - high.astype(jnp.float32)).astype(jnp.bfloat16)
                bdense[j, 0, k, here, u * blk:(u + 1) * blk] = high
                bdense[j, 1, k, here, u * blk:(u + 1) * blk] = low
            return carry

        lax.fori_loop(0, nb, per_chunk, 0)

    pieces = ops * col_blocks

    def selected(lev, j, pick):
        total = jnp.zeros((blk, wide), jnp.float32)
        for i in range(row_blocks):
            total += column[lev, j, i * blk:(i + 1) * blk, :].astype(jnp.float32) * one_hot(pick, i)
        return total.astype(jnp.bfloat16)

    wave = 2 * levels
    waves = levels + nb - 1

    def place_of(n):
        distance = (n // 2) % levels
        upper = n % 2
        j = n // wave - distance
        lev = z + distance * (2 * upper - 1)
        valid = (j >= 0) & (j < nb) & (lev >= 0) & (lev < levels) & (distance + 1 > upper)
        return lev, j, distance, valid

    def accumulate(owner, j, value):
        acc[j] += (jnp.dot(adense[owner, 0], value, preferred_element_type=jnp.float32)
                   + jnp.dot(adense[owner, 1], value, preferred_element_type=jnp.float32))

    def along(m):
        lev, j, distance, valid = place_of(m)

        @pl.when(valid)
        def _():
            @pl.when((distance == 0) & (j > 0))
            def _():
                pltpu.make_async_remote_copy(
                    src_ref=picks.at[1], dst_ref=column.at[z, j], send_sem=beta_send.at[0], recv_sem=beta_recv.at[jnp.maximum(j, 1) - 1],
                    device_id={"beta": c ^ 1}, device_id_type=MESH).wait_recv()

            @pl.when(distance > 0)
            def _():
                across_like = pltpu.make_async_remote_copy(
                    src_ref=column.at[lev, j], dst_ref=column.at[lev, j], send_sem=up_send.at[lev, j], recv_sem=column_recv.at[lev, j],
                    device_id={"alpha": partner}, device_id_type=MESH)
                across_like.wait_recv()

            owner = lev * PAIR + x
            chosen[lev, j] = selected(lev, j, small[na + owner])

            @pl.when((lev <= z) & (z < levels - 1))
            def _():
                up_copy(lev, j).start()

            @pl.when((lev >= z) & (z > 0))
            def _():
                down_copy(lev, j).start()

            across_copy(lev, j).start()

            @pl.when(m == 0)
            def _():
                build_a()

            accumulate(owner, j, selected(lev, j, small[owner]))

    def over(m):
        lev, j, distance, valid = place_of(m)

        @pl.when(valid)
        def _():
            across_copy(lev, j).wait_recv()
            accumulate(lev * PAIR + 1 - x, j, across[lev, j])

    steps = waves * wave
    tile = min(2, col_blocks) * blk

    def finish(j):
        inters = [acc[j, k * rows:(k + 1) * rows, :].astype(jnp.bfloat16) for k in range(ops)]

        def columns(n, carry):
            here = pl.ds(pl.multiple_of(n * tile, tile), tile)
            total = out_ref[:, here]
            for k in range(ops):
                for half in range(2):
                    total += lax.dot_general(inters[k], bdense[j, half, k, here, :], (((1,), (1,)), ((), ())),
                                             preferred_element_type=jnp.float32)
            out_ref[:, here] = total
            return carry

        lax.fori_loop(0, col_blocks * blk // tile, columns, 0)

    def step(m, carry):
        @pl.when(m < steps)
        def _():
            along(m)

        piece = m - wave

        @pl.when(piece == 0)
        def _():
            copy_b.wait()

        @pl.when((piece >= 0) & (piece < pieces))
        def _():
            build_b(piece)

        @pl.when(m >= wave)
        def _():
            over(m - wave)

        done = m // wave - levels

        @pl.when((m % wave == wave - 1) & (done >= 0))
        def _():
            finish(done)

        return carry

    lax.fori_loop(0, steps + wave, step, 0)

    for j in range(1, nb):
        beta_copy(j).wait_send()

    def drain(n, carry):
        lev = n // nb
        j = n % nb

        @pl.when((lev <= z) & (z < levels - 1))
        def _():
            up_copy(lev, j).wait_send()

        @pl.when((lev >= z) & (z > 0))
        def _():
            down_copy(lev, j).wait_send()

        across_copy(lev, j).wait_send()
        return carry

    lax.fori_loop(0, levels * nb, drain, 0)


def scratch_of(geometry, dtype):
    na, nb, ops, slots, blk, row_blocks, col_blocks = geometry
    levels = na // PAIR
    rows, cols, wide = row_blocks * blk, col_blocks * blk, FROM_B * blk
    return [
        ((ops, slots, rows, blk), dtype),
        ((ops, slots, cols, blk), dtype),
        ((levels, nb, rows, wide), dtype),
        ((levels, nb, blk, wide), dtype),
        ((levels, nb, blk, wide), dtype),
        ((na, 2, ops * rows, blk), dtype),
        ((nb, 2, ops, cols, wide), dtype),
        ((nb, ops * rows, wide), jnp.float32),
    ]


def scratch_bytes(geometry):
    total = 0
    for shape, dtype in scratch_of(geometry, jnp.bfloat16):
        size = jnp.dtype(dtype).itemsize
        for extent in shape:
            size *= extent
        total += size
    return total


def fused(geometry, coeffs, a_blocks, a_list, a_count, b_blocks, b_list, b_count):
    na, nb, ops, slots, blk, row_blocks, col_blocks = geometry
    levels = na // PAIR
    a_lists = jnp.transpose(a_list, (2, 0, 1))
    b_lists = jnp.transpose(b_list, (2, 0, 1))
    rows, cols = row_blocks * blk, col_blocks * blk
    dma = pltpu.SemaphoreType.DMA
    smem = pl.BlockSpec(memory_space=pltpu.SMEM)
    vmem = pl.BlockSpec(memory_space=pltpu.VMEM)
    picks, small = pl.pallas_call(
        functools.partial(pick_kernel, geometry),
        out_shape=(jax.ShapeDtypeStruct((nb, rows, FROM_B * blk), coeffs.dtype), jax.ShapeDtypeStruct((2 * na + nb,), jnp.int32)),
        in_specs=[smem, vmem, vmem],
        out_specs=(vmem, smem),
        name="pick_blocks",
    )(a_lists, b_lists, coeffs)
    return pl.pallas_call(
        functools.partial(sigma_kernel, geometry),
        out_shape=jax.ShapeDtypeStruct((rows, cols), jnp.float32),
        in_specs=[
            smem, smem, smem, smem, smem, vmem,
            pl.BlockSpec(memory_space=pl.ANY),
            pl.BlockSpec(memory_space=pl.ANY),
        ],
        out_specs=pl.BlockSpec(memory_space=pltpu.VMEM),
        scratch_shapes=[pltpu.VMEM(shape, dtype) for shape, dtype in scratch_of(geometry, coeffs.dtype)] + [
            dma((2,)), dma((nb - 1,)), dma((nb - 1,)), dma((levels, nb)), dma((levels, nb)), dma((levels, nb)),
            dma((levels, nb)), dma((levels, nb)),
        ],
        compiler_params=pltpu.CompilerParams(collective_id=0, has_side_effects=True, vmem_limit_bytes=VMEM_LIMIT),
        name="sigma_build",
    )(small, a_lists, a_count, b_lists, b_count, picks, jnp.transpose(a_blocks, (0, 2, 1, 3)), jnp.transpose(b_blocks, (0, 2, 1, 3)))


def arrange(entries, owners, per_owner, capacity):
    operators, total, list_slots = entries.shape
    flattened = entries.reshape(operators, owners, per_owner * list_slots)
    matches = flattened[..., None] == jnp.arange(total, dtype=jnp.int32)
    present = jnp.any(matches, axis=(0, 2)).reshape(owners, owners, per_owner).astype(jnp.int32)
    ranking = jnp.cumsum(present, axis=2)
    position = jnp.arange(capacity, dtype=jnp.int32) + 1
    chosen_bits = (present[..., None] == 1) & (ranking[..., None] == position)
    local_ids = jnp.arange(per_owner, dtype=jnp.int32)[None, None, :, None]
    wanted = jnp.sum(local_ids * chosen_bits.astype(jnp.int32), axis=2)
    return (wanted, ranking)


def locate(entries, ranking_here, per_owner, capacity):
    owner = entries // per_owner
    local_id = entries % per_owner
    return owner * capacity + ranking_here[owner, local_id] - 1


def pick_columns(pool_piece, index_piece):
    return pool_piece[:, index_piece]


def plain(coeffs, a_blocks, a_list, a_count, b_blocks, b_list, b_count):
    operators, local_rows, list_slots, block_size = a_blocks.shape
    local_cols = coeffs.shape[1]
    row_blocks = local_rows // block_size
    col_blocks = local_cols // block_size
    row_capacity = FROM_A
    col_capacity = FROM_B
    alpha_size = lax.axis_size("alpha")
    beta_size = lax.axis_size("beta")
    alpha_here = lax.axis_index("alpha")
    beta_here = lax.axis_index("beta")
    slot_ids = jnp.arange(list_slots, dtype=jnp.int32)
    alpha_mine = lax.dynamic_slice_in_dim(a_list, alpha_here * row_blocks, row_blocks, 1)
    alpha_counts = lax.dynamic_slice_in_dim(a_count, alpha_here * row_blocks, row_blocks, 1)
    alpha_valid = slot_ids < alpha_counts[..., None]
    alpha_kept = jnp.where(
        alpha_valid[:, :, None, :, None],
        a_blocks.reshape(operators, row_blocks, block_size, list_slots, block_size),
        jnp.zeros((), jnp.bfloat16),
    )
    wanted, ranking = arrange(a_list, alpha_size, row_blocks, row_capacity)
    outgoing = coeffs.reshape(row_blocks, block_size, local_cols)[wanted[:, alpha_here, :]]
    incoming = lax.all_to_all(outgoing, "alpha", split_axis=0, concat_axis=0, tiled=True)
    source_index = locate(alpha_mine, ranking[alpha_here], row_blocks, row_capacity)
    chosen = incoming.reshape(alpha_size * row_capacity, block_size, local_cols)[source_index]
    inter = jnp.einsum("kbrsi,kbsic->kbrc", alpha_kept, chosen, preferred_element_type=jnp.float32)
    inter = inter.astype(jnp.bfloat16).reshape(operators, local_rows, col_blocks, block_size)
    wanted_cols, ranking_cols = arrange(b_list, beta_size, col_blocks, col_capacity)
    outgoing_cols = inter[:, :, wanted_cols[:, beta_here, :], :]
    incoming_cols = lax.all_to_all(outgoing_cols, "beta", split_axis=2, concat_axis=2, tiled=True)
    beta_mine = lax.dynamic_slice_in_dim(b_list, beta_here * col_blocks, col_blocks, 1)
    beta_counts = lax.dynamic_slice_in_dim(b_count, beta_here * col_blocks, col_blocks, 1)
    beta_valid = slot_ids < beta_counts[..., None]
    beta_kept = jnp.where(
        beta_valid[:, :, None, :, None],
        b_blocks.reshape(operators, col_blocks, block_size, list_slots, block_size),
        jnp.zeros((), jnp.bfloat16),
    )
    source_cols = locate(beta_mine, ranking_cols[beta_here], col_blocks, col_capacity)
    pooled = incoming_cols.reshape(operators, local_rows, beta_size * col_capacity, block_size)
    picked = jax.vmap(pick_columns)(pooled, source_cols)
    sigma = jnp.einsum("kabsj,kbrsj->abr", picked, beta_kept, preferred_element_type=jnp.float32)
    return sigma.reshape(local_rows, local_cols)


def on_device(coeffs, a_blocks, a_list, a_count, b_blocks, b_list, b_count):
    operators, local_rows, list_slots, block_size = a_blocks.shape
    na, nb = lax.axis_size("alpha"), lax.axis_size("beta")
    geometry = (na, nb, operators, list_slots, block_size, local_rows // block_size, coeffs.shape[1] // block_size)
    fits = scratch_bytes(geometry) < VMEM_LIMIT * 3 // 4
    shaped = FROM_A == 1 and FROM_B == 2 and na % PAIR == 0 and nb & (nb - 1) == 0 and nb > 1
    build = functools.partial(fused, geometry) if fits and shaped else plain
    return build(coeffs, a_blocks, a_list, a_count, b_blocks, b_list, b_count)


def solution(mesh):
    in_specs = (
        P("alpha", "beta"),
        P(None, "alpha", None, None),
        P(),
        P(),
        P(None, "beta", None, None),
        P(),
        P(),
    )
    out_specs = P("alpha", "beta")
    return jax.shard_map(
        on_device, mesh=mesh, in_specs=in_specs, out_specs=out_specs, check_vma=False
    )
```

profile of v0, /device:TPU:0, one launch (start us, length us, event | category | flops | bytes accessed | tf_op | source)
XLA Modules:
  0.0 57.3 jit_solution(1372538321498061575)
XLA Ops:
  0.0 2.4 %pick_blocks.1 = (bf16[4,256,256]{2,1,0:T(8,128)(2,1)}, s32[20]{0:T(128)}) custom-call(s32[11,2,16]{2,1,0:T(2,128)} %bitcast.6, s32[11,2,32]{2,1,0:T(2,128)} %bitcast.8, bf16[256,1024]{1,0:T(8,128)(2,1)} %c_ref.1), custom_call_target="tpu_custom_call" | custom-call | tf_op jit(solution)/shard_map/pick_blocks/pallas_call | solution.py:339
  2.4 52.7 %sigma_build.1 = f32[256,1024]{1,0:T(8,128)} custom-call(s32[20]{0:T(128)} %get-tuple-element.7.small, s32[11,2,16]{2,1,0:T(2,128)} %bitcast.7, s32[2,16]{1,0:T(2,128)} %a_counts.1, s32[11,2,32]{2,1,0:T(2,128)} %bitcast.9, s32[2,32]{1,0:T(2,128)} %b_counts.1, bf16[4,256,256]{2,1,0:T(8,128)(2,1)} %get-tuple-element.8.picks, ...), custom_call_target="tpu_custom_call" | custom-call | tf_op jit(solution)/shard_map/sigma_build/pallas_call | solution.py:346
  55.0 2.3 %copy.9 = f32[256,1024]{1,0:T(8,128)} copy(f32[256,1024]{1,0:T(8,128)} %sigma_build.1) | data formatting | bytes 2097152
where the time goes:
time: 57.6 us; the launch traced here: 57.3 us
  Pallas kernels  55 us (95%)
  local copies, waits for them, and re-layouts  2.31 us (4%)
    pallas_call x1, Pallas kernels, fused(): pl.pallas_call(functools.partial(sigma_kernel, geometry), out_shape=jax.S...  52.7 us
    pallas_call x1, Pallas kernels, fused(): pl.pallas_call(functools.partial(pick_kernel, geometry), out_shape=(jax.S...  2.36 us
    unnamed x1, local copies, waits for them, and re-layouts  2.31 us

commit v1 on v0

v1 whole, which is shorter than its diff:
```python
import functools

import jax
import jax.numpy as jnp
from jax import lax
from jax.experimental import pallas as pl
from jax.experimental.pallas import tpu as pltpu
from jax.sharding import PartitionSpec as P

FROM_A = 1
FROM_B = 2
PAIR = 2
VMEM_LIMIT = 60 * 1024 * 1024
MESH = pl.DeviceIdType.MESH


def sigma_kernel(geometry, a_lists, a_counts, b_lists, b_counts, a_vec, b_vec, c_hbm, a_hbm, b_hbm, out_ref, cbuf, abuf, bbuf, picks, column, across, chosen,
                 adense, bdense, acc, small, local_sem, beta_send, beta_recv, column_recv, up_send, down_send, across_send, across_recv):
    na, nb, ops, slots, blk, row_blocks, col_blocks = geometry
    levels = na // PAIR
    rows = row_blocks * blk
    wide = FROM_B * blk
    a = lax.axis_index("alpha")
    c = lax.axis_index("beta")
    z = a // PAIR
    x = a % PAIR
    partner = a + 1 - 2 * x

    copies_c = [pltpu.make_async_copy(c_hbm.at[:, b * blk:(b + 1) * blk], cbuf.at[b], local_sem.at[2 + b]) for b in range(col_blocks)]
    copy_a = pltpu.make_async_copy(a_hbm, abuf, local_sem.at[0])
    copy_b = pltpu.make_async_copy(b_hbm, bbuf, local_sem.at[1])
    for copy in copies_c:
        copy.start()
    copy_a.start()
    copy_b.start()

    barrier = pltpu.get_barrier_semaphore()
    for j in range(1, nb):
        pl.semaphore_signal(barrier, inc=1, device_id={"beta": c ^ j}, device_id_type=MESH)
    pl.semaphore_signal(barrier, inc=1, device_id={"alpha": partner}, device_id_type=MESH)

    @pl.when(z < levels - 1)
    def _():
        pl.semaphore_signal(barrier, inc=1, device_id={"alpha": a + PAIR}, device_id_type=MESH)

    @pl.when(z > 0)
    def _():
        pl.semaphore_signal(barrier, inc=1, device_id={"alpha": a - PAIR}, device_id_type=MESH)

    lists = b_vec[...]
    lane = lax.broadcasted_iota(jnp.int32, (1, nb * col_blocks), 1)

    def extremes(receiver, owner):
        local = lists - owner * col_blocks
        hit = (local >= 0) & (local < col_blocks)
        rows_here = (lane >= receiver * col_blocks) & (lane < (receiver + 1) * col_blocks)
        low = jnp.min(jnp.min(jnp.where(hit, local, col_blocks), axis=0), axis=0, keepdims=True)
        high = jnp.max(jnp.max(jnp.where(hit, local, 0), axis=0), axis=0, keepdims=True)
        low = jnp.min(jnp.where(rows_here, low, col_blocks))
        high = jnp.max(jnp.where(rows_here, high, 0))
        return jnp.where(low < col_blocks, low, 0), high

    spans = [extremes(c ^ j, c) for j in range(nb)]
    for copy in copies_c:
        copy.wait()
    for j in range(nb):
        for u, block in enumerate(spans[j]):
            piece = cbuf[block]
            if j == 0:
                column[z, 0, :, u * blk:(u + 1) * blk] = piece
            else:
                picks[j - 1, :, u * blk:(u + 1) * blk] = piece

    rows_list = a_vec[...]
    row_lane = lax.broadcasted_iota(jnp.int32, (1, na * row_blocks), 1)

    def row_pick(receiver, owner):
        local = rows_list - owner * row_blocks
        hit = (local >= 0) & (local < row_blocks)
        rows_here = (row_lane >= receiver * row_blocks) & (row_lane < (receiver + 1) * row_blocks)
        high = jnp.max(jnp.max(jnp.where(hit, local, 0), axis=0), axis=0, keepdims=True)
        return jnp.max(jnp.where(rows_here, high, 0))

    for lev in range(levels):
        small[lev] = row_pick(a, lev * PAIR + x)
        small[levels + lev] = row_pick(partner, lev * PAIR + x)
    for owner in range(nb):
        small[2 * levels + owner] = extremes(c, owner)[0]

    neighbours = nb + jnp.where(z < levels - 1, 1, 0) + jnp.where(z > 0, 1, 0)
    pl.semaphore_wait(barrier, neighbours)

    def beta_copy(j):
        return pltpu.make_async_remote_copy(
            src_ref=picks.at[j - 1], dst_ref=column.at[z, j], send_sem=beta_send.at[j - 1], recv_sem=beta_recv.at[j - 1],
            device_id={"beta": c ^ j}, device_id_type=MESH)

    def up_copy(lev, j):
        return pltpu.make_async_remote_copy(
            src_ref=column.at[lev, j], dst_ref=column.at[lev, j], send_sem=up_send.at[lev, j], recv_sem=column_recv.at[lev, j],
            device_id={"alpha": a + PAIR}, device_id_type=MESH)

    def down_copy(lev, j):
        return pltpu.make_async_remote_copy(
            src_ref=column.at[lev, j], dst_ref=column.at[lev, j], send_sem=down_send.at[lev, j], recv_sem=column_recv.at[lev, j],
            device_id={"alpha": a - PAIR}, device_id_type=MESH)

    def across_copy(lev, j):
        return pltpu.make_async_remote_copy(
            src_ref=chosen.at[lev, j], dst_ref=across.at[lev, j], send_sem=across_send.at[lev, j], recv_sem=across_recv.at[lev, j],
            device_id={"alpha": partner}, device_id_type=MESH)

    def one_hot(value, place):
        gap = value - place
        return (1 - jnp.minimum(jnp.maximum(gap, -gap), 1)).astype(jnp.float32)

    def at_most(slot, count):
        return jnp.minimum(jnp.maximum(count - slot, 0), 1)

    def selected(lev, j, pick):
        total = jnp.zeros((blk, wide), jnp.float32)
        for i in range(row_blocks):
            total += column[lev, j, i * blk:(i + 1) * blk, :].astype(jnp.float32) * one_hot(pick, i)
        return total.astype(jnp.bfloat16)

    def offer(lev, j):
        chosen[lev, j] = selected(lev, j, small[levels + lev])
        across_copy(lev, j).start()

    def own_sends(j):
        @pl.when(z < levels - 1)
        def _():
            up_copy(z, j).start()

        @pl.when(z > 0)
        def _():
            down_copy(z, j).start()

        offer(z, j)

    own_sends(0)
    for j in range(1, nb):
        beta_copy(j).start()

    tall = 32

    def dense(load, codes, places, put):
        def tile(t, carry):
            here = pl.multiple_of(t * tall, tall)
            totals = [jnp.zeros((tall, blk), jnp.float32) for _ in range(places)]
            for s in range(slots):
                value = load(s, here)
                for p in range(places):
                    totals[p] += value * one_hot(codes[s], p)
            for p in range(places):
                high = totals[p].astype(jnp.bfloat16)
                put(p, here, high, (totals[p] - high.astype(jnp.float32)).astype(jnp.bfloat16))
            return carry

        lax.fori_loop(0, blk // tall, tile, 0)

    def build_a(piece):
        k = piece // row_blocks
        i = piece % row_blocks
        codes = []
        for s in range(slots):
            entry = a_lists[s, k, a * row_blocks + i]
            owner = lax.div(entry, row_blocks)
            upper = owner - 2 * lax.div(owner, 2)
            place = owner - upper + jnp.maximum(upper - x, x - upper)
            codes.append((place + 1) * at_most(s, a_counts[k, a * row_blocks + i]) - 1)

        def load(s, here):
            return abuf[k, s, pl.ds(i * blk + here, tall), :].astype(jnp.float32)

        def put(p, here, high, low):
            at = pl.ds(k * rows + i * blk + here, tall)
            side = p % PAIR
            adense[p // PAIR, 0, at, side * blk:(side + 1) * blk] = high
            adense[p // PAIR, 1, at, side * blk:(side + 1) * blk] = low

        dense(load, codes, na, put)

    def build_b(piece):
        k = piece // col_blocks
        r = piece % col_blocks
        codes = []
        for s in range(slots):
            entry = b_lists[s, k, c * col_blocks + r]
            owner = lax.div(entry, col_blocks)
            gap = entry - owner * col_blocks - small[2 * levels + owner]
            place = (owner ^ c) * FROM_B + jnp.minimum(jnp.maximum(gap, -gap), 1)
            codes.append((place + 1) * at_most(s, b_counts[k, c * col_blocks + r]) - 1)

        def load(s, here):
            return bbuf[k, s, pl.ds(r * blk + here, tall), :].astype(jnp.float32)

        def put(p, here, high, low):
            at = pl.ds(r * blk + here, tall)
            u = p % FROM_B
            bdense[p // FROM_B, 0, k, at, u * blk:(u + 1) * blk] = high
            bdense[p // FROM_B, 1, k, at, u * blk:(u + 1) * blk] = low

        dense(load, codes, nb * FROM_B, put)

    a_pieces = ops * row_blocks
    pieces = ops * col_blocks

    def build_some(first, count):
        def one(n, carry):
            @pl.when(n < pieces)
            def _():
                build_b(n)
            return carry

        lax.fori_loop(first, first + count, one, 0)

    def beta_wait(j):
        pltpu.make_async_remote_copy(
            src_ref=picks.at[j - 1], dst_ref=column.at[z, j], send_sem=beta_send.at[j - 1], recv_sem=beta_recv.at[j - 1],
            device_id={"beta": c ^ j}, device_id_type=MESH).wait_recv()

    acc[...] = jnp.zeros_like(acc)
    out_ref[...] = jnp.zeros_like(out_ref)
    copy_a.wait()

    def one_a(n, carry):
        build_a(n)
        return carry

    lax.fori_loop(0, a_pieces // 2, one_a, 0)
    built = 0
    for j in range(1, nb):
        beta_wait(j)
        own_sends(j)
        if j == 1:
            lax.fori_loop(a_pieces // 2, a_pieces, one_a, 0)
            copy_b.wait()
        build_some(built, 3)
        built += 3

    def combine(lev, j):
        across_copy(lev, j).wait_recv()
        value = jnp.concatenate([selected(lev, j, small[lev]), across[lev, j]], axis=0)
        acc[j] += (jnp.dot(adense[lev, 0], value, preferred_element_type=jnp.float32)
                   + jnp.dot(adense[lev, 1], value, preferred_element_type=jnp.float32))

    tile = min(2, col_blocks) * blk

    def finish(j):
        inters = [acc[j, k * rows:(k + 1) * rows, :].astype(jnp.bfloat16) for k in range(ops)]

        def columns(n, carry):
            here = pl.ds(pl.multiple_of(n * tile, tile), tile)
            total = out_ref[:, here]
            for k in range(ops):
                for half in range(2):
                    total += lax.dot_general(inters[k], bdense[j, half, k, here, :], (((1,), (1,)), ((), ())),
                                             preferred_element_type=jnp.float32)
            out_ref[:, here] = total
            return carry

        lax.fori_loop(0, col_blocks * blk // tile, columns, 0)

    steps = (levels - 1) * nb
    farthest = jnp.maximum(z, levels - 1 - z)

    def arrive(lev, j, below):
        pltpu.make_async_remote_copy(
            src_ref=column.at[lev, j], dst_ref=column.at[lev, j], send_sem=up_send.at[lev, j], recv_sem=column_recv.at[lev, j],
            device_id={"alpha": partner}, device_id_type=MESH).wait_recv()
        if below:
            @pl.when(z < levels - 1)
            def _():
                up_copy(lev, j).start()
        else:
            @pl.when(z > 0)
            def _():
                down_copy(lev, j).start()

        offer(lev, j)

    def step(i, carry):
        j = i % nb
        distance = i // nb + 1

        @pl.when((i < steps) & (z - distance >= 0))
        def _():
            arrive(z - distance, j, True)

        @pl.when((i < steps) & (z + distance < levels))
        def _():
            arrive(z + distance, j, False)

        @pl.when(i < nb)
        def _():
            combine(z, j)

        before = jnp.maximum(i - 1, 0)
        j_before = before % nb
        distance_before = before // nb + 1

        @pl.when((i > 0) & (z - distance_before >= 0))
        def _():
            combine(z - distance_before, j_before)

        @pl.when((i > 0) & (z + distance_before < levels))
        def _():
            combine(z + distance_before, j_before)

        done = i - 1 - (farthest - 1) * nb
        build_some(built + 2 * i, 2)

        @pl.when((done >= 0) & (done < nb))
        def _():
            finish(done)

        return carry

    lax.fori_loop(0, steps + 1, step, 0)

    for j in range(1, nb):
        beta_copy(j).wait_send()

    def drain(n, carry):
        lev = n // nb
        j = n % nb

        @pl.when((lev <= z) & (z < levels - 1))
        def _():
            up_copy(lev, j).wait_send()

        @pl.when((lev >= z) & (z > 0))
        def _():
            down_copy(lev, j).wait_send()

        across_copy(lev, j).wait_send()
        return carry

    lax.fori_loop(0, levels * nb, drain, 0)


def scratch_of(geometry, dtype):
    na, nb, ops, slots, blk, row_blocks, col_blocks = geometry
    levels = na // PAIR
    rows, cols, wide = row_blocks * blk, col_blocks * blk, FROM_B * blk
    return [
        ((col_blocks, rows, blk), dtype),
        ((ops, slots, rows, blk), dtype),
        ((ops, slots, cols, blk), dtype),
        ((nb - 1, rows, wide), dtype),
        ((levels, nb, rows, wide), dtype),
        ((levels, nb, blk, wide), dtype),
        ((levels, nb, blk, wide), dtype),
        ((levels, 2, ops * rows, PAIR * blk), dtype),
        ((nb, 2, ops, cols, wide), dtype),
        ((nb, ops * rows, wide), jnp.float32),
    ]


def scratch_bytes(geometry):
    total = 0
    for shape, dtype in scratch_of(geometry, jnp.bfloat16):
        size = jnp.dtype(dtype).itemsize
        for extent in shape:
            size *= extent
        total += size
    return total


def fused(geometry, coeffs, a_blocks, a_list, a_count, b_blocks, b_list, b_count):
    na, nb, ops, slots, blk, row_blocks, col_blocks = geometry
    levels = na // PAIR
    a_lists = jnp.transpose(a_list, (2, 0, 1))
    b_lists = jnp.transpose(b_list, (2, 0, 1))
    rows, cols = row_blocks * blk, col_blocks * blk
    dma = pltpu.SemaphoreType.DMA
    smem = pl.BlockSpec(memory_space=pltpu.SMEM)
    vmem = pl.BlockSpec(memory_space=pltpu.VMEM)
    return pl.pallas_call(
        functools.partial(sigma_kernel, geometry),
        out_shape=jax.ShapeDtypeStruct((rows, cols), jnp.float32),
        in_specs=[
            smem, smem, smem, smem, vmem, vmem,
            pl.BlockSpec(memory_space=pl.ANY),
            pl.BlockSpec(memory_space=pl.ANY),
            pl.BlockSpec(memory_space=pl.ANY),
        ],
        out_specs=pl.BlockSpec(memory_space=pltpu.VMEM),
        scratch_shapes=[pltpu.VMEM(shape, dtype) for shape, dtype in scratch_of(geometry, coeffs.dtype)] + [
            pltpu.SMEM((2 * levels + nb,), jnp.int32),
            dma((2 + col_blocks,)), dma((nb - 1,)), dma((nb - 1,)), dma((levels, nb)), dma((levels, nb)), dma((levels, nb)),
            dma((levels, nb)), dma((levels, nb)),
        ],
        compiler_params=pltpu.CompilerParams(collective_id=0, has_side_effects=True, vmem_limit_bytes=VMEM_LIMIT),
        name="sigma_build",
    )(a_lists, a_count, b_lists, b_count, a_lists, b_lists, coeffs, jnp.transpose(a_blocks, (0, 2, 1, 3)), jnp.transpose(b_blocks, (0, 2, 1, 3)))


def arrange(entries, owners, per_owner, capacity):
    operators, total, list_slots = entries.shape
    flattened = entries.reshape(operators, owners, per_owner * list_slots)
    matches = flattened[..., None] == jnp.arange(total, dtype=jnp.int32)
    present = jnp.any(matches, axis=(0, 2)).reshape(owners, owners, per_owner).astype(jnp.int32)
    ranking = jnp.cumsum(present, axis=2)
    position = jnp.arange(capacity, dtype=jnp.int32) + 1
    chosen_bits = (present[..., None] == 1) & (ranking[..., None] == position)
    local_ids = jnp.arange(per_owner, dtype=jnp.int32)[None, None, :, None]
    wanted = jnp.sum(local_ids * chosen_bits.astype(jnp.int32), axis=2)
    return (wanted, ranking)


def locate(entries, ranking_here, per_owner, capacity):
    owner = entries // per_owner
    local_id = entries % per_owner
    return owner * capacity + ranking_here[owner, local_id] - 1


def pick_columns(pool_piece, index_piece):
    return pool_piece[:, index_piece]


def plain(coeffs, a_blocks, a_list, a_count, b_blocks, b_list, b_count):
    operators, local_rows, list_slots, block_size = a_blocks.shape
    local_cols = coeffs.shape[1]
    row_blocks = local_rows // block_size
    col_blocks = local_cols // block_size
    row_capacity = FROM_A
    col_capacity = FROM_B
    alpha_size = lax.axis_size("alpha")
    beta_size = lax.axis_size("beta")
    alpha_here = lax.axis_index("alpha")
    beta_here = lax.axis_index("beta")
    slot_ids = jnp.arange(list_slots, dtype=jnp.int32)
    alpha_mine = lax.dynamic_slice_in_dim(a_list, alpha_here * row_blocks, row_blocks, 1)
    alpha_counts = lax.dynamic_slice_in_dim(a_count, alpha_here * row_blocks, row_blocks, 1)
    alpha_valid = slot_ids < alpha_counts[..., None]
    alpha_kept = jnp.where(
        alpha_valid[:, :, None, :, None],
        a_blocks.reshape(operators, row_blocks, block_size, list_slots, block_size),
        jnp.zeros((), jnp.bfloat16),
    )
    wanted, ranking = arrange(a_list, alpha_size, row_blocks, row_capacity)
    outgoing = coeffs.reshape(row_blocks, block_size, local_cols)[wanted[:, alpha_here, :]]
    incoming = lax.all_to_all(outgoing, "alpha", split_axis=0, concat_axis=0, tiled=True)
    source_index = locate(alpha_mine, ranking[alpha_here], row_blocks, row_capacity)
    chosen = incoming.reshape(alpha_size * row_capacity, block_size, local_cols)[source_index]
    inter = jnp.einsum("kbrsi,kbsic->kbrc", alpha_kept, chosen, preferred_element_type=jnp.float32)
    inter = inter.astype(jnp.bfloat16).reshape(operators, local_rows, col_blocks, block_size)
    wanted_cols, ranking_cols = arrange(b_list, beta_size, col_blocks, col_capacity)
    outgoing_cols = inter[:, :, wanted_cols[:, beta_here, :], :]
    incoming_cols = lax.all_to_all(outgoing_cols, "beta", split_axis=2, concat_axis=2, tiled=True)
    beta_mine = lax.dynamic_slice_in_dim(b_list, beta_here * col_blocks, col_blocks, 1)
    beta_counts = lax.dynamic_slice_in_dim(b_count, beta_here * col_blocks, col_blocks, 1)
    beta_valid = slot_ids < beta_counts[..., None]
    beta_kept = jnp.where(
        beta_valid[:, :, None, :, None],
        b_blocks.reshape(operators, col_blocks, block_size, list_slots, block_size),
        jnp.zeros((), jnp.bfloat16),
    )
    source_cols = locate(beta_mine, ranking_cols[beta_here], col_blocks, col_capacity)
    pooled = incoming_cols.reshape(operators, local_rows, beta_size * col_capacity, block_size)
    picked = jax.vmap(pick_columns)(pooled, source_cols)
    sigma = jnp.einsum("kabsj,kbrsj->abr", picked, beta_kept, preferred_element_type=jnp.float32)
    return sigma.reshape(local_rows, local_cols)


def on_device(coeffs, a_blocks, a_list, a_count, b_blocks, b_list, b_count):
    operators, local_rows, list_slots, block_size = a_blocks.shape
    na, nb = lax.axis_size("alpha"), lax.axis_size("beta")
    geometry = (na, nb, operators, list_slots, block_size, local_rows // block_size, coeffs.shape[1] // block_size)
    fits = scratch_bytes(geometry) < VMEM_LIMIT * 3 // 4
    shaped = FROM_A == 1 and FROM_B == 2 and na % PAIR == 0 and na > PAIR and nb & (nb - 1) == 0 and nb > 1
    build = functools.partial(fused, geometry) if fits and shaped else plain
    return build(coeffs, a_blocks, a_list, a_count, b_blocks, b_list, b_count)


def solution(mesh):
    in_specs = (
        P("alpha", "beta"),
        P(None, "alpha", None, None),
        P(),
        P(),
        P(None, "beta", None, None),
        P(),
        P(),
    )
    out_specs = P("alpha", "beta")
    return jax.shard_map(
        on_device, mesh=mesh, in_specs=in_specs, out_specs=out_specs, check_vma=False
    )
```

time: 57.6 us -> 53.9 us (0.936)
  Pallas kernels: 55 us -> 51.4 us
    pallas_call x1 -> x0, Pallas kernels: 2.36 us -> none  [fused(): pl.pallas_call(functools.partial(pick_kernel, geometry), out_shape=(jax.S...]
    pallas_call x1, Pallas kernels: 52.7 us -> 51.4 us  [fused(): pl.pallas_call(functools.partial(sigma_kernel, geometry), out_shape=jax.S...]
where the time goes in v1:
time: 53.9 us; the launch traced here: 53.7 us
  Pallas kernels  51.4 us (95%)
  local copies, waits for them, and re-layouts  2.31 us (4%)
    pallas_call x1, Pallas kernels, fused(): pl.pallas_call(functools.partial(sigma_kernel, geometry), out_shape=jax.S...  51.4 us
    unnamed x1, local copies, waits for them, and re-layouts  2.31 us

profile of v1, /device:TPU:0, one launch (start us, length us, event | category | flops | bytes accessed | tf_op | source)
XLA Modules:
  0.0 53.7 jit_solution(10491942181967187815)
XLA Ops:
  0.0 51.4 %sigma_build.1 = f32[256,1024]{1,0:T(8,128)} custom-call(s32[11,2,16]{2,1,0:T(2,128)} %bitcast.6, s32[2,16]{1,0:T(2,128)} %a_counts.1, s32[11,2,32]{2,1,0:T(2,128)} %bitcast.8, s32[2,32]{1,0:T(2,128)} %b_counts.1, s32[11,2,16]{2,1,0:T(2,128)} %bitcast.7, s32[11,2,32]{2,1,0:T(2,128)} %bitcast.9, bf16[256,1024]{1,0:T(8,128)(2,1)} %c_hbm.1, ...), custom_call_target="tpu_custom_call" | custom-call | tf_op jit(solution)/shard_map/sigma_build/pallas_call | solution.py:380
  51.4 2.3 %copy.9 = f32[256,1024]{1,0:T(8,128)} copy(f32[256,1024]{1,0:T(8,128)} %sigma_build.1) | data formatting | bytes 2097152

commit v2 on v1

--- a/solution.py
+++ b/solution.py
@@ -15,7 +15,8 @@
 
 
 def sigma_kernel(geometry, a_lists, a_counts, b_lists, b_counts, a_vec, b_vec, c_hbm, a_hbm, b_hbm, out_ref, cbuf, abuf, bbuf, picks, column, across, chosen,
-                 adense, bdense, acc, small, local_sem, beta_send, beta_recv, column_recv, up_send, down_send, across_send, across_recv):
+                 straight, tail, adense, bdense, acc, small, local_sem, beta_send, beta_recv, column_recv, up_send, down_send, across_send, across_recv,
+                 straight_send, tail_recv):
     na, nb, ops, slots, blk, row_blocks, col_blocks = geometry
     levels = na // PAIR
     rows = row_blocks * blk
@@ -86,6 +87,11 @@
         small[levels + lev] = row_pick(partner, lev * PAIR + x)
     for owner in range(nb):
         small[2 * levels + owner] = extremes(c, owner)[0]
+    far = jnp.where(z == levels - 2, levels - 1, 0)
+    opposite = levels - 1 - far
+    for side in range(PAIR):
+        small[2 * levels + nb + side] = row_pick(far * PAIR + (x + side) % PAIR, opposite * PAIR + x)
+    out_ref[...] = jnp.zeros_like(out_ref)
 
     neighbours = nb + jnp.where(z < levels - 1, 1, 0) + jnp.where(z > 0, 1, 0)
     pl.semaphore_wait(barrier, neighbours)
@@ -142,22 +148,18 @@
     for j in range(1, nb):
         beta_copy(j).start()
 
-    tall = 32
-
-    def dense(load, codes, places, put):
-        def tile(t, carry):
-            here = pl.multiple_of(t * tall, tall)
-            totals = [jnp.zeros((tall, blk), jnp.float32) for _ in range(places)]
+    def dense(load, codes, groups, per_group, put):
+        def group(g, carry):
+            totals = [jnp.zeros((blk, blk), jnp.float32) for _ in range(per_group)]
             for s in range(slots):
-                value = load(s, here)
-                for p in range(places):
-                    totals[p] += value * one_hot(codes[s], p)
-            for p in range(places):
-                high = totals[p].astype(jnp.bfloat16)
-                put(p, here, high, (totals[p] - high.astype(jnp.float32)).astype(jnp.bfloat16))
+                value = load(s)
+                for p in range(per_group):
+                    totals[p] += value * jnp.where(codes[s] == g * per_group + p, 1.0, 0.0)
+            for p in range(per_group):
+                put(g, p, totals[p])
             return carry
 
-        lax.fori_loop(0, blk // tall, tile, 0)
+        lax.fori_loop(0, groups, group, 0)
 
     def build_a(piece):
         k = piece // row_blocks
@@ -170,16 +172,16 @@
             place = owner - upper + jnp.maximum(upper - x, x - upper)
             codes.append((place + 1) * at_most(s, a_counts[k, a * row_blocks + i]) - 1)
 
-        def load(s, here):
-            return abuf[k, s, pl.ds(i * blk + here, tall), :].astype(jnp.float32)
-
-        def put(p, here, high, low):
-            at = pl.ds(k * rows + i * blk + here, tall)
-            side = p % PAIR
-            adense[p // PAIR, 0, at, side * blk:(side + 1) * blk] = high
-            adense[p // PAIR, 1, at, side * blk:(side + 1) * blk] = low
-
-        dense(load, codes, na, put)
+        def load(s):
+            return abuf[k, s, pl.ds(i * blk, blk), :].astype(jnp.float32)
+
+        def put(g, p, total):
+            at = pl.ds(k * rows + i * blk, blk)
+            high = total.astype(jnp.bfloat16)
+            adense[g, at, p * blk:(p + 1) * blk] = high
+            adense[g, at, (PAIR + p) * blk:(PAIR + p + 1) * blk] = (total - high.astype(jnp.float32)).astype(jnp.bfloat16)
+
+        dense(load, codes, levels, PAIR, put)
 
     def build_b(piece):
         k = piece // col_blocks
@@ -192,16 +194,13 @@
             place = (owner ^ c) * FROM_B + jnp.minimum(jnp.maximum(gap, -gap), 1)
             codes.append((place + 1) * at_most(s, b_counts[k, c * col_blocks + r]) - 1)
 
-        def load(s, here):
-            return bbuf[k, s, pl.ds(r * blk + here, tall), :].astype(jnp.float32)
-
-        def put(p, here, high, low):
-            at = pl.ds(r * blk + here, tall)
-            u = p % FROM_B
-            bdense[p // FROM_B, 0, k, at, u * blk:(u + 1) * blk] = high
-            bdense[p // FROM_B, 1, k, at, u * blk:(u + 1) * blk] = low
-
-        dense(load, codes, nb * FROM_B, put)
+        def load(s):
+            return bbuf[k, s, pl.ds(r * blk, blk), :].astype(jnp.float32)
+
+        def put(g, p, total):
+            bdense[g, k, pl.ds(r * blk, blk), p * blk:(p + 1) * blk] = total.astype(jnp.bfloat16)
+
+        dense(load, codes, nb, FROM_B, put)
 
     a_pieces = ops * row_blocks
     pieces = ops * col_blocks
@@ -220,8 +219,6 @@
             src_ref=picks.at[j - 1], dst_ref=column.at[z, j], send_sem=beta_send.at[j - 1], recv_sem=beta_recv.at[j - 1],
             device_id={"beta": c ^ j}, device_id_type=MESH).wait_recv()
 
-    acc[...] = jnp.zeros_like(acc)
-    out_ref[...] = jnp.zeros_like(out_ref)
     copy_a.wait()
 
     def one_a(n, carry):
@@ -236,14 +233,18 @@
         if j == 1:
             lax.fori_loop(a_pieces // 2, a_pieces, one_a, 0)
             copy_b.wait()
-        build_some(built, 3)
-        built += 3
+        if j < nb - 1:
+            build_some(built, 2 * j)
+            built += 2 * j
+
+    def product(lev, j, mine):
+        across_copy(lev, j).wait_recv()
+        other = across[lev, j]
+        value = jnp.concatenate([mine, other, mine, other], axis=0)
+        return jnp.dot(adense[lev], value, preferred_element_type=jnp.float32)
 
     def combine(lev, j):
-        across_copy(lev, j).wait_recv()
-        value = jnp.concatenate([selected(lev, j, small[lev]), across[lev, j]], axis=0)
-        acc[j] += (jnp.dot(adense[lev, 0], value, preferred_element_type=jnp.float32)
-                   + jnp.dot(adense[lev, 1], value, preferred_element_type=jnp.float32))
+        acc[j] += product(lev, j, selected(lev, j, small[lev]))
 
     tile = min(2, col_blocks) * blk
 
@@ -254,70 +255,95 @@
             here = pl.ds(pl.multiple_of(n * tile, tile), tile)
             total = out_ref[:, here]
             for k in range(ops):
-                for half in range(2):
-                    total += lax.dot_general(inters[k], bdense[j, half, k, here, :], (((1,), (1,)), ((), ())),
-                                             preferred_element_type=jnp.float32)
+                total += lax.dot_general(inters[k], bdense[j, k, here, :], (((1,), (1,)), ((), ())),
+                                         preferred_element_type=jnp.float32)
             out_ref[:, here] = total
             return carry
 
         lax.fori_loop(0, col_blocks * blk // tile, columns, 0)
 
-    steps = (levels - 1) * nb
-    farthest = jnp.maximum(z, levels - 1 - z)
+    def straight_copy(j):
+        return pltpu.make_async_remote_copy(
+            src_ref=straight.at[0, j], dst_ref=tail.at[j], send_sem=straight_send.at[0, j], recv_sem=tail_recv.at[j],
+            device_id={"alpha": far * PAIR + x}, device_id_type=MESH)
+
+    def diagonal_copy(j):
+        return pltpu.make_async_remote_copy(
+            src_ref=straight.at[1, j], dst_ref=across.at[opposite, j], send_sem=straight_send.at[1, j], recv_sem=across_recv.at[opposite, j],
+            device_id={"alpha": far * PAIR + 1 - x}, device_id_type=MESH)
 
     def arrive(lev, j, below):
         pltpu.make_async_remote_copy(
             src_ref=column.at[lev, j], dst_ref=column.at[lev, j], send_sem=up_send.at[lev, j], recv_sem=column_recv.at[lev, j],
             device_id={"alpha": partner}, device_id_type=MESH).wait_recv()
+        last = (z == levels - 2) & (lev == 0) if below else (z == 1) & (lev == levels - 1)
+
+        @pl.when(last)
+        def _():
+            straight[1, j] = selected(lev, j, small[2 * levels + nb + 1])
+            diagonal_copy(j).start()
+            straight[0, j] = selected(lev, j, small[2 * levels + nb])
+            straight_copy(j).start()
+
         if below:
-            @pl.when(z < levels - 1)
+            @pl.when((z < levels - 1) & jnp.logical_not(last))
             def _():
                 up_copy(lev, j).start()
         else:
-            @pl.when(z > 0)
+            @pl.when((z > 0) & jnp.logical_not(last))
             def _():
                 down_copy(lev, j).start()
 
         offer(lev, j)
+
+    relayed = (levels - 2) * nb
+    at_end = (z == 0) | (z == levels - 1)
 
     def step(i, carry):
         j = i % nb
         distance = i // nb + 1
 
-        @pl.when((i < steps) & (z - distance >= 0))
+        @pl.when((i < relayed) & (z - distance >= 0))
         def _():
             arrive(z - distance, j, True)
 
-        @pl.when((i < steps) & (z + distance < levels))
+        @pl.when((i < relayed) & (z + distance < levels))
         def _():
             arrive(z + distance, j, False)
 
         @pl.when(i < nb)
         def _():
-            combine(z, j)
+            acc[j] = product(z, j, selected(z, j, small[z]))
 
         before = jnp.maximum(i - 1, 0)
         j_before = before % nb
         distance_before = before // nb + 1
 
-        @pl.when((i > 0) & (z - distance_before >= 0))
+        @pl.when((i > 0) & (i <= relayed) & (z - distance_before >= 0))
         def _():
             combine(z - distance_before, j_before)
 
-        @pl.when((i > 0) & (z + distance_before < levels))
+        @pl.when((i > 0) & (i <= relayed) & (z + distance_before < levels))
         def _():
             combine(z + distance_before, j_before)
 
-        done = i - 1 - (farthest - 1) * nb
         build_some(built + 2 * i, 2)
 
-        @pl.when((done >= 0) & (done < nb))
-        def _():
-            finish(done)
+        @pl.when(i >= relayed)
+        def _():
+            @pl.when(at_end)
+            def _():
+                pltpu.make_async_remote_copy(
+                    src_ref=straight.at[0, j], dst_ref=tail.at[j], send_sem=straight_send.at[0, j], recv_sem=tail_recv.at[j],
+                    device_id={"alpha": partner}, device_id_type=MESH).wait_recv()
+                lev = levels - 1 - z
+                acc[j] += product(lev, j, tail[j])
+
+            finish(j)
 
         return carry
 
-    lax.fori_loop(0, steps + 1, step, 0)
+    lax.fori_loop(0, relayed + nb, step, 0)
 
     for j in range(1, nb):
         beta_copy(j).wait_send()
@@ -325,16 +351,26 @@
     def drain(n, carry):
         lev = n // nb
         j = n % nb
-
-        @pl.when((lev <= z) & (z < levels - 1))
+        up_last = (z == levels - 2) & (lev == 0)
+        down_last = (z == 1) & (lev == levels - 1)
+
+        @pl.when((lev <= z) & (z < levels - 1) & jnp.logical_not(up_last))
         def _():
             up_copy(lev, j).wait_send()
 
-        @pl.when((lev >= z) & (z > 0))
+        @pl.when((lev >= z) & (z > 0) & jnp.logical_not(down_last))
         def _():
             down_copy(lev, j).wait_send()
 
-        across_copy(lev, j).wait_send()
+        @pl.when(up_last | down_last)
+        def _():
+            straight_copy(j).wait_send()
+            diagonal_copy(j).wait_send()
+
+        @pl.when(jnp.logical_not(at_end & (lev == levels - 1 - z)))
+        def _():
+            across_copy(lev, j).wait_send()
+
         return carry
 
     lax.fori_loop(0, levels * nb, drain, 0)
@@ -352,8 +388,10 @@
         ((levels, nb, rows, wide), dtype),
         ((levels, nb, blk, wide), dtype),
         ((levels, nb, blk, wide), dtype),
-        ((levels, 2, ops * rows, PAIR * blk), dtype),
-        ((nb, 2, ops, cols, wide), dtype),
+        ((PAIR, nb, blk, wide), dtype),
+        ((nb, blk, wide), dtype),
+        ((levels, ops * rows, 2 * PAIR * blk), dtype),
+        ((nb, ops, cols, wide), dtype),
         ((nb, ops * rows, wide), jnp.float32),
     ]
 
@@ -388,9 +426,9 @@
         ],
         out_specs=pl.BlockSpec(memory_space=pltpu.VMEM),
         scratch_shapes=[pltpu.VMEM(shape, dtype) for shape, dtype in scratch_of(geometry, coeffs.dtype)] + [
-            pltpu.SMEM((2 * levels + nb,), jnp.int32),
+            pltpu.SMEM((2 * levels + nb + PAIR,), jnp.int32),
             dma((2 + col_blocks,)), dma((nb - 1,)), dma((nb - 1,)), dma((levels, nb)), dma((levels, nb)), dma((levels, nb)),
-            dma((levels, nb)), dma((levels, nb)),
+            dma((levels, nb)), dma((levels, nb)), dma((PAIR, nb)), dma((nb,)),
         ],
         compiler_params=pltpu.CompilerParams(collective_id=0, has_side_effects=True, vmem_limit_bytes=VMEM_LIMIT),
         name="sigma_build",
@@ -470,7 +508,7 @@
     na, nb = lax.axis_size("alpha"), lax.axis_size("beta")
     geometry = (na, nb, operators, list_slots, block_size, local_rows // block_size, coeffs.shape[1] // block_size)
     fits = scratch_bytes(geometry) < VMEM_LIMIT * 3 // 4
-    shaped = FROM_A == 1 and FROM_B == 2 and na % PAIR == 0 and na > PAIR and nb & (nb - 1) == 0 and nb > 1
+    shaped = FROM_A == 1 and FROM_B == 2 and na % PAIR == 0 and na > 3 * PAIR and nb & (nb - 1) == 0 and nb > 1
     build = functools.partial(fused, geometry) if fits and shaped else plain
     return build(coeffs, a_blocks, a_list, a_count, b_blocks, b_list, b_count)
 

time: 53.9 us -> 46.9 us (0.87)
  Pallas kernels: 51.4 us -> 44.3 us
    pallas_call x1, Pallas kernels: 51.4 us -> 44.3 us  [fused(): pl.pallas_call(functools.partial(sigma_kernel, geometry), out_shape=jax.S...]
where the time goes in v2:
time: 46.9 us; the launch traced here: 46.6 us
  Pallas kernels  44.3 us (94%)
  local copies, waits for them, and re-layouts  2.31 us (5%)
    pallas_call x1, Pallas kernels, fused(): pl.pallas_call(functools.partial(sigma_kernel, geometry), out_shape=jax.S...  44.3 us
    unnamed x1, local copies, waits for them, and re-layouts  2.31 us

profile of v2, /device:TPU:0, one launch (start us, length us, event | category | flops | bytes accessed | tf_op | source)
XLA Modules:
  0.0 46.6 jit_solution(1224271183585775715)
XLA Ops:
  0.0 44.3 %sigma_build.1 = f32[256,1024]{1,0:T(8,128)} custom-call(s32[11,2,16]{2,1,0:T(2,128)} %bitcast.6, s32[2,16]{1,0:T(2,128)} %a_counts.1, s32[11,2,32]{2,1,0:T(2,128)} %bitcast.8, s32[2,32]{1,0:T(2,128)} %b_counts.1, s32[11,2,16]{2,1,0:T(2,128)} %bitcast.7, s32[11,2,32]{2,1,0:T(2,128)} %bitcast.9, bf16[256,1024]{1,0:T(8,128)(2,1)} %c_hbm.1, ...), custom_call_target="tpu_custom_call" | custom-call | tf_op jit(solution)/shard_map/sigma_build/pallas_call | solution.py:418
  44.3 2.3 %copy.9 = f32[256,1024]{1,0:T(8,128)} copy(f32[256,1024]{1,0:T(8,128)} %sigma_build.1) | data formatting | bytes 2097152

commit v3 on v2

--- a/solution.py
+++ b/solution.py
@@ -11,11 +11,12 @@
 FROM_B = 2
 PAIR = 2
 VMEM_LIMIT = 60 * 1024 * 1024
+KERNEL_LIMIT = 40 * 1024 * 1024
 MESH = pl.DeviceIdType.MESH
 
 
-def sigma_kernel(geometry, a_lists, a_counts, b_lists, b_counts, a_vec, b_vec, c_hbm, a_hbm, b_hbm, out_ref, cbuf, abuf, bbuf, picks, column, across, chosen,
-                 straight, tail, adense, bdense, acc, small, local_sem, beta_send, beta_recv, column_recv, up_send, down_send, across_send, across_recv,
+def sigma_kernel(geometry, a_lists_hbm, a_counts_hbm, b_lists_hbm, b_counts_hbm, c_hbm, a_hbm, b_hbm, out_ref, a_lists, a_counts, b_lists, b_counts, a_vec, b_vec, cbuf, abuf, bbuf, picks, column, across, chosen,
+                 straight, tail, adense, bdense, acc, small, table_sem, local_sem, beta_send, beta_recv, column_recv, up_send, down_send, across_send, across_recv,
                  straight_send, tail_recv):
     na, nb, ops, slots, blk, row_blocks, col_blocks = geometry
     levels = na // PAIR
@@ -27,14 +28,6 @@
     x = a % PAIR
     partner = a + 1 - 2 * x
 
-    copies_c = [pltpu.make_async_copy(c_hbm.at[:, b * blk:(b + 1) * blk], cbuf.at[b], local_sem.at[2 + b]) for b in range(col_blocks)]
-    copy_a = pltpu.make_async_copy(a_hbm, abuf, local_sem.at[0])
-    copy_b = pltpu.make_async_copy(b_hbm, bbuf, local_sem.at[1])
-    for copy in copies_c:
-        copy.start()
-    copy_a.start()
-    copy_b.start()
-
     barrier = pltpu.get_barrier_semaphore()
     for j in range(1, nb):
         pl.semaphore_signal(barrier, inc=1, device_id={"beta": c ^ j}, device_id_type=MESH)
@@ -47,6 +40,18 @@
     @pl.when(z > 0)
     def _():
         pl.semaphore_signal(barrier, inc=1, device_id={"alpha": a - PAIR}, device_id_type=MESH)
+
+    tables = [(b_lists_hbm, b_vec), (a_lists_hbm, a_vec), (a_lists_hbm, a_lists), (a_counts_hbm, a_counts), (b_lists_hbm, b_lists), (b_counts_hbm, b_counts)]
+    copies_t = [pltpu.make_async_copy(source, target, table_sem.at[n]) for n, (source, target) in enumerate(tables)]
+    copies_c = [pltpu.make_async_copy(c_hbm.at[:, b * blk:(b + 1) * blk], cbuf.at[b], local_sem.at[2 + b]) for b in range(col_blocks)]
+    copy_a = pltpu.make_async_copy(a_hbm, abuf, local_sem.at[0])
+    copy_b = pltpu.make_async_copy(b_hbm, bbuf, local_sem.at[1])
+    for copy in copies_t + copies_c:
+        copy.start()
+    copy_a.start()
+    copy_b.start()
+    for copy in copies_t:
+        copy.wait()
 
     lists = b_vec[...]
     lane = lax.broadcasted_iota(jnp.int32, (1, nb * col_blocks), 1)
@@ -413,26 +418,23 @@
     b_lists = jnp.transpose(b_list, (2, 0, 1))
     rows, cols = row_blocks * blk, col_blocks * blk
     dma = pltpu.SemaphoreType.DMA
-    smem = pl.BlockSpec(memory_space=pltpu.SMEM)
-    vmem = pl.BlockSpec(memory_space=pltpu.VMEM)
-    return pl.pallas_call(
+    held = pl.pallas_call(
         functools.partial(sigma_kernel, geometry),
-        out_shape=jax.ShapeDtypeStruct((rows, cols), jnp.float32),
-        in_specs=[
-            smem, smem, smem, smem, vmem, vmem,
-            pl.BlockSpec(memory_space=pl.ANY),
-            pl.BlockSpec(memory_space=pl.ANY),
-            pl.BlockSpec(memory_space=pl.ANY),
-        ],
+        out_shape=pltpu.VMEM((rows, cols), jnp.float32),
+        in_specs=[pl.BlockSpec(memory_space=pltpu.HBM)] * 7,
         out_specs=pl.BlockSpec(memory_space=pltpu.VMEM),
-        scratch_shapes=[pltpu.VMEM(shape, dtype) for shape, dtype in scratch_of(geometry, coeffs.dtype)] + [
+        scratch_shapes=[
+            pltpu.SMEM(a_lists.shape, jnp.int32), pltpu.SMEM(a_count.shape, jnp.int32), pltpu.SMEM(b_lists.shape, jnp.int32),
+            pltpu.SMEM(b_count.shape, jnp.int32), pltpu.VMEM(a_lists.shape, jnp.int32), pltpu.VMEM(b_lists.shape, jnp.int32),
+        ] + [pltpu.VMEM(shape, dtype) for shape, dtype in scratch_of(geometry, coeffs.dtype)] + [
             pltpu.SMEM((2 * levels + nb + PAIR,), jnp.int32),
-            dma((2 + col_blocks,)), dma((nb - 1,)), dma((nb - 1,)), dma((levels, nb)), dma((levels, nb)), dma((levels, nb)),
+            dma((6,)), dma((2 + col_blocks,)), dma((nb - 1,)), dma((nb - 1,)), dma((levels, nb)), dma((levels, nb)), dma((levels, nb)),
             dma((levels, nb)), dma((levels, nb)), dma((PAIR, nb)), dma((nb,)),
         ],
-        compiler_params=pltpu.CompilerParams(collective_id=0, has_side_effects=True, vmem_limit_bytes=VMEM_LIMIT),
+        compiler_params=pltpu.CompilerParams(collective_id=0, has_side_effects=True, vmem_limit_bytes=KERNEL_LIMIT),
         name="sigma_build",
-    )(a_lists, a_count, b_lists, b_count, a_lists, b_lists, coeffs, jnp.transpose(a_blocks, (0, 2, 1, 3)), jnp.transpose(b_blocks, (0, 2, 1, 3)))
+    )(*[pltpu.with_memory_space_constraint(v, pltpu.HBM) for v in (a_lists, a_count, b_lists, b_count, coeffs, jnp.transpose(a_blocks, (0, 2, 1, 3)), jnp.transpose(b_blocks, (0, 2, 1, 3)))])
+    return held
 
 
 def arrange(entries, owners, per_owner, capacity):

time: 46.9 us -> 43.7 us (0.932)
  Pallas kernels: 44.3 us -> 42.6 us
  local copies, waits for them, and re-layouts: 2.31 us -> 0.97 us
    pallas_call x1, Pallas kernels: 44.3 us -> 42.6 us  [fused(): pl.pallas_call(functools.partial(sigma_kernel, geometry), out_shape=pltpu...]
    unnamed x1, local copies, waits for them, and re-layouts: 2.31 us -> 0.97 us
where the time goes in v3:
time: 43.7 us; the launch traced here: 43.5 us
  Pallas kernels  42.6 us (97%)
  local copies, waits for them, and re-layouts  0.97 us (2%)
    pallas_call x1, Pallas kernels, fused(): pl.pallas_call(functools.partial(sigma_kernel, geometry), out_shape=pltpu...  42.6 us
    unnamed x1, local copies, waits for them, and re-layouts  0.97 us

profile of v3, /device:TPU:0, one launch (start us, length us, event | category | flops | bytes accessed | tf_op | source)
XLA Modules:
  0.0 43.5 jit_solution(11664031560850238272)
XLA Ops:
  0.0 42.6 %sigma_build.1 = f32[256,1024]{1,0:T(8,128)S(1)} custom-call(s32[11,2,16]{2,1,0:T(2,128)} %bitcast.6, s32[2,16]{1,0:T(2,128)} %a_counts_hbm.1, s32[11,2,32]{2,1,0:T(2,128)} %bitcast.7, s32[2,32]{1,0:T(2,128)} %b_counts_hbm.1, bf16[256,1024]{1,0:T(8,128)(2,1)} %c_hbm.1, bf16[2,11,256,128]{3,2,1,0:T(8,128)(2,1)} %bitcast.5, bf16[2,11,1024,128]{3,2,1,0:T(8,128)(2,1)} %bitcast.4), custom_call_target="tpu_custom_call" | custom-call | tf_op jit(solution)/shard_map/sigma_build/pallas_call | solution.py:421
  42.6 1.0 %copy.9 = f32[256,1024]{1,0:T(8,128)} copy(f32[256,1024]{1,0:T(8,128)S(1)} %sigma_build.1) | data formatting | bytes 2097152

commit v4 on v3

--- a/solution.py
+++ b/solution.py
@@ -15,7 +15,7 @@
 MESH = pl.DeviceIdType.MESH
 
 
-def sigma_kernel(geometry, a_lists_hbm, a_counts_hbm, b_lists_hbm, b_counts_hbm, c_hbm, a_hbm, b_hbm, out_ref, a_lists, a_counts, b_lists, b_counts, a_vec, b_vec, cbuf, abuf, bbuf, picks, column, across, chosen,
+def sigma_kernel(geometry, a_lists_hbm, a_counts_hbm, b_lists_hbm, b_counts_hbm, c_hbm, a_hbm, b_hbm, out_ref, last_ref, last_b_ref, a_lists, a_counts, b_lists, b_counts, a_vec, b_vec, cbuf, abuf, bbuf, picks, column, across, chosen,
                  straight, tail, adense, bdense, acc, small, table_sem, local_sem, beta_send, beta_recv, column_recv, up_send, down_send, across_send, across_recv,
                  straight_send, tail_recv):
     na, nb, ops, slots, blk, row_blocks, col_blocks = geometry
@@ -50,8 +50,7 @@
         copy.start()
     copy_a.start()
     copy_b.start()
-    for copy in copies_t:
-        copy.wait()
+    copies_t[0].wait()
 
     lists = b_vec[...]
     lane = lax.broadcasted_iota(jnp.int32, (1, nb * col_blocks), 1)
@@ -77,6 +76,60 @@
             else:
                 picks[j - 1, :, u * blk:(u + 1) * blk] = piece
 
+    neighbours = nb + jnp.where(z < levels - 1, 1, 0) + jnp.where(z > 0, 1, 0)
+    pl.semaphore_wait(barrier, neighbours)
+
+    def beta_copy(j):
+        return pltpu.make_async_remote_copy(
+            src_ref=picks.at[j - 1], dst_ref=column.at[z, j], send_sem=beta_send.at[j - 1], recv_sem=beta_recv.at[j - 1],
+            device_id={"beta": c ^ j}, device_id_type=MESH)
+
+    def up_copy(lev, j):
+        return pltpu.make_async_remote_copy(
+            src_ref=column.at[lev, j], dst_ref=column.at[lev, j], send_sem=up_send.at[lev, j], recv_sem=column_recv.at[lev, j],
+            device_id={"alpha": a + PAIR}, device_id_type=MESH)
+
+    def down_copy(lev, j):
+        return pltpu.make_async_remote_copy(
+            src_ref=column.at[lev, j], dst_ref=column.at[lev, j], send_sem=down_send.at[lev, j], recv_sem=column_recv.at[lev, j],
+            device_id={"alpha": a - PAIR}, device_id_type=MESH)
+
+    def across_copy(lev, j):
+        return pltpu.make_async_remote_copy(
+            src_ref=chosen.at[lev, j], dst_ref=across.at[lev, j], send_sem=across_send.at[lev, j], recv_sem=across_recv.at[lev, j],
+            device_id={"alpha": partner}, device_id_type=MESH)
+
+    def one_hot(value, place):
+        gap = value - place
+        return (1 - jnp.minimum(jnp.maximum(gap, -gap), 1)).astype(jnp.float32)
+
+    def at_most(slot, count):
+        return jnp.minimum(jnp.maximum(count - slot, 0), 1)
+
+    def selected(lev, j, pick):
+        total = jnp.zeros((blk, wide), jnp.float32)
+        for i in range(row_blocks):
+            total += column[lev, j, i * blk:(i + 1) * blk, :].astype(jnp.float32) * one_hot(pick, i)
+        return total.astype(jnp.bfloat16)
+
+    def offer(lev, j):
+        chosen[lev, j] = selected(lev, j, small[levels + lev])
+        across_copy(lev, j).start()
+
+    def own_relays(j):
+        @pl.when(z < levels - 1)
+        def _():
+            up_copy(z, j).start()
+
+        @pl.when(z > 0)
+        def _():
+            down_copy(z, j).start()
+
+    own_relays(0)
+    for j in range(1, nb):
+        beta_copy(j).start()
+    for copy in copies_t[1:]:
+        copy.wait()
     rows_list = a_vec[...]
     row_lane = lax.broadcasted_iota(jnp.int32, (1, na * row_blocks), 1)
 
@@ -98,60 +151,7 @@
         small[2 * levels + nb + side] = row_pick(far * PAIR + (x + side) % PAIR, opposite * PAIR + x)
     out_ref[...] = jnp.zeros_like(out_ref)
 
-    neighbours = nb + jnp.where(z < levels - 1, 1, 0) + jnp.where(z > 0, 1, 0)
-    pl.semaphore_wait(barrier, neighbours)
-
-    def beta_copy(j):
-        return pltpu.make_async_remote_copy(
-            src_ref=picks.at[j - 1], dst_ref=column.at[z, j], send_sem=beta_send.at[j - 1], recv_sem=beta_recv.at[j - 1],
-            device_id={"beta": c ^ j}, device_id_type=MESH)
-
-    def up_copy(lev, j):
-        return pltpu.make_async_remote_copy(
-            src_ref=column.at[lev, j], dst_ref=column.at[lev, j], send_sem=up_send.at[lev, j], recv_sem=column_recv.at[lev, j],
-            device_id={"alpha": a + PAIR}, device_id_type=MESH)
-
-    def down_copy(lev, j):
-        return pltpu.make_async_remote_copy(
-            src_ref=column.at[lev, j], dst_ref=column.at[lev, j], send_sem=down_send.at[lev, j], recv_sem=column_recv.at[lev, j],
-            device_id={"alpha": a - PAIR}, device_id_type=MESH)
-
-    def across_copy(lev, j):
-        return pltpu.make_async_remote_copy(
-            src_ref=chosen.at[lev, j], dst_ref=across.at[lev, j], send_sem=across_send.at[lev, j], recv_sem=across_recv.at[lev, j],
-            device_id={"alpha": partner}, device_id_type=MESH)
-
-    def one_hot(value, place):
-        gap = value - place
-        return (1 - jnp.minimum(jnp.maximum(gap, -gap), 1)).astype(jnp.float32)
-
-    def at_most(slot, count):
-        return jnp.minimum(jnp.maximum(count - slot, 0), 1)
-
-    def selected(lev, j, pick):
-        total = jnp.zeros((blk, wide), jnp.float32)
-        for i in range(row_blocks):
-            total += column[lev, j, i * blk:(i + 1) * blk, :].astype(jnp.float32) * one_hot(pick, i)
-        return total.astype(jnp.bfloat16)
-
-    def offer(lev, j):
-        chosen[lev, j] = selected(lev, j, small[levels + lev])
-        across_copy(lev, j).start()
-
-    def own_sends(j):
-        @pl.when(z < levels - 1)
-        def _():
-            up_copy(z, j).start()
-
-        @pl.when(z > 0)
-        def _():
-            down_copy(z, j).start()
-
-        offer(z, j)
-
-    own_sends(0)
-    for j in range(1, nb):
-        beta_copy(j).start()
+    offer(z, 0)
 
     def dense(load, codes, groups, per_group, put):
         def group(g, carry):
@@ -234,7 +234,8 @@
     built = 0
     for j in range(1, nb):
         beta_wait(j)
-        own_sends(j)
+        own_relays(j)
+        offer(z, j)
         if j == 1:
             lax.fori_loop(a_pieces // 2, a_pieces, one_a, 0)
             copy_b.wait()
@@ -304,7 +305,7 @@
     relayed = (levels - 2) * nb
     at_end = (z == 0) | (z == levels - 1)
 
-    def step(i, carry):
+    def step(i, carry, final=False):
         j = i % nb
         distance = i // nb + 1
 
@@ -344,14 +345,15 @@
                 lev = levels - 1 - z
                 acc[j] += product(lev, j, tail[j])
 
-            finish(j)
+            if final:
+                for k in range(ops):
+                    last_ref[k] = acc[j, k * rows:(k + 1) * rows, :].astype(jnp.bfloat16)
+            else:
+                finish(j)
 
         return carry
 
-    lax.fori_loop(0, relayed + nb, step, 0)
-
-    for j in range(1, nb):
-        beta_copy(j).wait_send()
+    lax.fori_loop(0, relayed + nb - 1, step, 0)
 
     def drain(n, carry):
         lev = n // nb
@@ -378,7 +380,32 @@
 
         return carry
 
-    lax.fori_loop(0, levels * nb, drain, 0)
+    def drain_all():
+        for j in range(1, nb):
+            beta_copy(j).wait_send()
+        lax.fori_loop(0, levels * nb, drain, 0)
+
+    @pl.when(at_end)
+    def _():
+        drain_all()
+
+    last_b_ref[...] = bdense[nb - 1]
+    step(relayed + nb - 1, 0, True)
+
+    @pl.when(jnp.logical_not(at_end))
+    def _():
+        drain_all()
+
+
+def close_kernel(tile, part, last, last_b, out_hbm, staged, sems):
+    copies = []
+    for n in range(part.shape[1] // tile):
+        here = slice(n * tile, (n + 1) * tile)
+        staged[n] = part[:, here] + sum(lax.dot_general(last[k], last_b[k, here, :], (((1,), (1,)), ((), ())), preferred_element_type=jnp.float32) for k in range(last.shape[0]))
+        copies.append(pltpu.make_async_copy(staged.at[n], out_hbm.at[:, here], sems.at[n]))
+        copies[-1].start()
+    for copy in copies:
+        copy.wait()
 
 
 def scratch_of(geometry, dtype):
@@ -418,11 +445,12 @@
     b_lists = jnp.transpose(b_list, (2, 0, 1))
     rows, cols = row_blocks * blk, col_blocks * blk
     dma = pltpu.SemaphoreType.DMA
+    vmem = pl.BlockSpec(memory_space=pltpu.VMEM)
     held = pl.pallas_call(
         functools.partial(sigma_kernel, geometry),
-        out_shape=pltpu.VMEM((rows, cols), jnp.float32),
+        out_shape=(pltpu.VMEM((rows, cols), jnp.float32), pltpu.VMEM((ops, rows, FROM_B * blk), coeffs.dtype), pltpu.VMEM((ops, cols, FROM_B * blk), coeffs.dtype)),
         in_specs=[pl.BlockSpec(memory_space=pltpu.HBM)] * 7,
-        out_specs=pl.BlockSpec(memory_space=pltpu.VMEM),
+        out_specs=(vmem, vmem, vmem),
         scratch_shapes=[
             pltpu.SMEM(a_lists.shape, jnp.int32), pltpu.SMEM(a_count.shape, jnp.int32), pltpu.SMEM(b_lists.shape, jnp.int32),
             pltpu.SMEM(b_count.shape, jnp.int32), pltpu.VMEM(a_lists.shape, jnp.int32), pltpu.VMEM(b_lists.shape, jnp.int32),
@@ -434,7 +462,16 @@
         compiler_params=pltpu.CompilerParams(collective_id=0, has_side_effects=True, vmem_limit_bytes=KERNEL_LIMIT),
         name="sigma_build",
     )(*[pltpu.with_memory_space_constraint(v, pltpu.HBM) for v in (a_lists, a_count, b_lists, b_count, coeffs, jnp.transpose(a_blocks, (0, 2, 1, 3)), jnp.transpose(b_blocks, (0, 2, 1, 3)))])
-    return held
+    tile = min(2, cols // blk) * blk
+    return pl.pallas_call(
+        functools.partial(close_kernel, tile),
+        out_shape=jax.ShapeDtypeStruct((rows, cols), jnp.float32),
+        in_specs=[vmem, vmem, vmem],
+        out_specs=pl.BlockSpec(memory_space=pltpu.HBM),
+        scratch_shapes=[pltpu.VMEM((cols // tile, rows, tile), jnp.float32), dma((cols // tile,))],
+        compiler_params=pltpu.CompilerParams(vmem_limit_bytes=8 * 1024 * 1024),
+        name="close_sigma",
+    )(*held)
 
 
 def arrange(entries, owners, per_owner, capacity):

time: 43.7 us -> 42.5 us (0.973)
  local copies, waits for them, and re-layouts: 0.97 us -> 0 us
    unnamed x1 -> x0, local copies, waits for them, and re-layouts: 0.97 us -> none
    pallas_call x1 -> x2, Pallas kernels: 42.6 us -> 42.4 us  [the longest x1 41 us: fused(): pl.pallas_call(functools.partial(sigma_kernel, geometry), out_shape=(pltp...]
where the time goes in v4:
time: 42.5 us; the launch traced here: 42.4 us
  Pallas kernels  42.4 us (100%)
    pallas_call x1, Pallas kernels, fused(): pl.pallas_call(functools.partial(sigma_kernel, geometry), out_shape=(pltp...  41 us
    pallas_call x1, Pallas kernels, fused(): pl.pallas_call(functools.partial(close_kernel, tile), out_shape=jax.Shape...  1.34 us

profile of v4, /device:TPU:0, one launch (start us, length us, event | category | flops | bytes accessed | tf_op | source)
XLA Modules:
  0.0 42.4 jit_solution(3824468119527862199)
XLA Ops:
  0.0 41.0 %sigma_build.1 = (f32[256,1024]{1,0:T(8,128)S(1)}, bf16[2,256,256]{2,1,0:T(8,128)(2,1)S(1)}, bf16[2,1024,256]{2,1,0:T(8,128)(2,1)S(1)}) custom-call(s32[11,2,16]{2,1,0:T(2,128)} %bitcast.6, s32[2,16]{1,0:T(2,128)} %a_counts_hbm.1, s32[11,2,32]{2,1,0:T(2,128)} %bitcast.7, s32[2,32]{1,0:T(2,128)} %b_counts_hbm.1, bf16[256,1024]{1,0:T(8,128)(2,1)} %c_hbm.1, ...), custom_call_target="tpu_custom_call" | custom-call | tf_op jit(solution)/shard_map/sigma_build/pallas_call | solution.py:449
  41.0 1.3 %close_sigma.1 = f32[256,1024]{1,0:T(8,128)} custom-call(f32[256,1024]{1,0:T(8,128)S(1)} %get-tuple-element.8.part, bf16[2,256,256]{2,1,0:T(8,128)(2,1)S(1)} %get-tuple-element.9.last, bf16[2,1024,256]{2,1,0:T(8,128)(2,1)S(1)} %get-tuple-element.10.last_b), custom_call_target="tpu_custom_call" | custom-call | tf_op jit(solution)/shard_map/close_sigma/pallas_call | solution.py:466

commit v5 on v4

--- a/solution.py
+++ b/solution.py
@@ -10,6 +10,8 @@
 FROM_A = 1
 FROM_B = 2
 PAIR = 2
+LAG = 3
+CORES = 2
 VMEM_LIMIT = 60 * 1024 * 1024
 KERNEL_LIMIT = 40 * 1024 * 1024
 MESH = pl.DeviceIdType.MESH
@@ -17,7 +19,7 @@
 
 def sigma_kernel(geometry, a_lists_hbm, a_counts_hbm, b_lists_hbm, b_counts_hbm, c_hbm, a_hbm, b_hbm, out_ref, last_ref, last_b_ref, a_lists, a_counts, b_lists, b_counts, a_vec, b_vec, cbuf, abuf, bbuf, picks, column, across, chosen,
                  straight, tail, adense, bdense, acc, small, table_sem, local_sem, beta_send, beta_recv, column_recv, up_send, down_send, across_send, across_recv,
-                 straight_send, tail_recv):
+                 straight_send, tail_recv, aside_send):
     na, nb, ops, slots, blk, row_blocks, col_blocks = geometry
     levels = na // PAIR
     rows = row_blocks * blk
@@ -278,6 +280,25 @@
             src_ref=straight.at[1, j], dst_ref=across.at[opposite, j], send_sem=straight_send.at[1, j], recv_sem=across_recv.at[opposite, j],
             device_id={"alpha": far * PAIR + 1 - x}, device_id_type=MESH)
 
+    lightened = (z == 1) & (c < CORES)
+    forwards = (z == 1) & (c >= CORES) & (c < 2 * CORES)
+    beside = jnp.where(c < CORES, c + CORES, jnp.where(c < 2 * CORES, c - CORES, c))
+
+    def aside_copy():
+        return pltpu.make_async_remote_copy(
+            src_ref=straight.at[1 - x, 0], dst_ref=tail.at[0], send_sem=aside_send.at[0], recv_sem=tail_recv.at[0],
+            device_id={"beta": beside}, device_id_type=MESH)
+
+    def forward_crossing():
+        return pltpu.make_async_remote_copy(
+            src_ref=tail.at[0], dst_ref=across.at[levels - 1, 0], send_sem=aside_send.at[1], recv_sem=across_recv.at[levels - 1, 0],
+            device_id={"alpha": a - 1, "beta": beside}, device_id_type=MESH)
+
+    def forward_direct():
+        return pltpu.make_async_remote_copy(
+            src_ref=tail.at[0], dst_ref=tail.at[0], send_sem=aside_send.at[1], recv_sem=tail_recv.at[0],
+            device_id={"alpha": a - PAIR, "beta": beside}, device_id_type=MESH)
+
     def arrive(lev, j, below):
         pltpu.make_async_remote_copy(
             src_ref=column.at[lev, j], dst_ref=column.at[lev, j], send_sem=up_send.at[lev, j], recv_sem=column_recv.at[lev, j],
@@ -287,9 +308,24 @@
         @pl.when(last)
         def _():
             straight[1, j] = selected(lev, j, small[2 * levels + nb + 1])
-            diagonal_copy(j).start()
             straight[0, j] = selected(lev, j, small[2 * levels + nb])
-            straight_copy(j).start()
+            if below:
+                diagonal_copy(j).start()
+                straight_copy(j).start()
+            else:
+                turned = lightened & (j == 0)
+
+                @pl.when(turned)
+                def _():
+                    aside_copy().start()
+
+                @pl.when(jnp.logical_not(turned & (x == 0)))
+                def _():
+                    diagonal_copy(j).start()
+
+                @pl.when(jnp.logical_not(turned & (x == 1)))
+                def _():
+                    straight_copy(j).start()
 
         if below:
             @pl.when((z < levels - 1) & jnp.logical_not(last))
@@ -309,6 +345,18 @@
         j = i % nb
         distance = i // nb + 1
 
+        @pl.when((i == relayed - nb + 1) & forwards)
+        def _():
+            aside_copy().wait_recv()
+
+            @pl.when(x == 0)
+            def _():
+                forward_crossing().start()
+
+            @pl.when(x == 1)
+            def _():
+                forward_direct().start()
+
         @pl.when((i < relayed) & (z - distance >= 0))
         def _():
             arrive(z - distance, j, True)
@@ -317,23 +365,32 @@
         def _():
             arrive(z + distance, j, False)
 
-        @pl.when(i < nb)
-        def _():
-            acc[j] = product(z, j, selected(z, j, small[z]))
-
-        before = jnp.maximum(i - 1, 0)
+        own = jnp.maximum(i - 1, 0) % nb
+
+        @pl.when((i > 0) & (i <= nb))
+        def _():
+            acc[own] = product(z, own, selected(z, own, small[z]))
+
+        before = jnp.maximum(i - LAG, 0)
         j_before = before % nb
         distance_before = before // nb + 1
 
-        @pl.when((i > 0) & (i <= relayed) & (z - distance_before >= 0))
+        @pl.when((i >= LAG) & (i < relayed + LAG) & (z - distance_before >= 0))
         def _():
             combine(z - distance_before, j_before)
 
-        @pl.when((i > 0) & (i <= relayed) & (z + distance_before < levels))
+        @pl.when((i >= LAG) & (i < relayed + LAG) & (z + distance_before < levels))
         def _():
             combine(z + distance_before, j_before)
 
         build_some(built + 2 * i, 2)
+
+
+        early = i - (relayed + LAG - nb)
+
+        @pl.when((early >= 0) & (early < nb - 1) & jnp.logical_not(at_end))
+        def _():
+            finish(early)
 
         @pl.when(i >= relayed)
         def _():
@@ -343,13 +400,22 @@
                     src_ref=straight.at[0, j], dst_ref=tail.at[j], send_sem=straight_send.at[0, j], recv_sem=tail_recv.at[j],
                     device_id={"alpha": partner}, device_id_type=MESH).wait_recv()
                 lev = levels - 1 - z
-                acc[j] += product(lev, j, tail[j])
+                total = acc[j] + product(lev, j, tail[j])
+                if final:
+                    for k in range(ops):
+                        last_ref[k] = total[k * rows:(k + 1) * rows].astype(jnp.bfloat16)
+                else:
+                    acc[j] = total
 
             if final:
-                for k in range(ops):
-                    last_ref[k] = acc[j, k * rows:(k + 1) * rows, :].astype(jnp.bfloat16)
+                @pl.when(jnp.logical_not(at_end))
+                def _():
+                    for k in range(ops):
+                        last_ref[k] = acc[j, k * rows:(k + 1) * rows, :].astype(jnp.bfloat16)
             else:
-                finish(j)
+                @pl.when(at_end)
+                def _():
+                    finish(j)
 
         return carry
 
@@ -371,8 +437,23 @@
 
         @pl.when(up_last | down_last)
         def _():
-            straight_copy(j).wait_send()
-            diagonal_copy(j).wait_send()
+            turned = lightened & (j == 0)
+
+            @pl.when(turned)
+            def _():
+                aside_copy().wait_send()
+
+            @pl.when(jnp.logical_not(turned & (x == 1)))
+            def _():
+                straight_copy(j).wait_send()
+
+            @pl.when(jnp.logical_not(turned & (x == 0)))
+            def _():
+                diagonal_copy(j).wait_send()
+
+            @pl.when(forwards & (j == 0))
+            def _():
+                forward_direct().wait_send()
 
         @pl.when(jnp.logical_not(at_end & (lev == levels - 1 - z)))
         def _():
@@ -457,12 +538,12 @@
         ] + [pltpu.VMEM(shape, dtype) for shape, dtype in scratch_of(geometry, coeffs.dtype)] + [
             pltpu.SMEM((2 * levels + nb + PAIR,), jnp.int32),
             dma((6,)), dma((2 + col_blocks,)), dma((nb - 1,)), dma((nb - 1,)), dma((levels, nb)), dma((levels, nb)), dma((levels, nb)),
-            dma((levels, nb)), dma((levels, nb)), dma((PAIR, nb)), dma((nb,)),
+            dma((levels, nb)), dma((levels, nb)), dma((PAIR, nb)), dma((nb,)), dma((2,)),
         ],
         compiler_params=pltpu.CompilerParams(collective_id=0, has_side_effects=True, vmem_limit_bytes=KERNEL_LIMIT),
         name="sigma_build",
     )(*[pltpu.with_memory_space_constraint(v, pltpu.HBM) for v in (a_lists, a_count, b_lists, b_count, coeffs, jnp.transpose(a_blocks, (0, 2, 1, 3)), jnp.transpose(b_blocks, (0, 2, 1, 3)))])
-    tile = min(2, cols // blk) * blk
+    tile = cols // 2
     return pl.pallas_call(
         functools.partial(close_kernel, tile),
         out_shape=jax.ShapeDtypeStruct((rows, cols), jnp.float32),
@@ -547,7 +628,7 @@
     na, nb = lax.axis_size("alpha"), lax.axis_size("beta")
     geometry = (na, nb, operators, list_slots, block_size, local_rows // block_size, coeffs.shape[1] // block_size)
     fits = scratch_bytes(geometry) < VMEM_LIMIT * 3 // 4
-    shaped = FROM_A == 1 and FROM_B == 2 and na % PAIR == 0 and na > 3 * PAIR and nb & (nb - 1) == 0 and nb > 1
+    shaped = FROM_A == 1 and FROM_B == 2 and na % PAIR == 0 and na > 3 * PAIR and nb & (nb - 1) == 0 and nb >= 2 * CORES
     build = functools.partial(fused, geometry) if fits and shaped else plain
     return build(coeffs, a_blocks, a_list, a_count, b_blocks, b_list, b_count)
 

time: 42.5 us -> 41.7 us (0.981)
  the two profiles are of different devices: /device:TPU:0 before, /device:TPU:4 now
where the time goes in v5:
time: 41.7 us; the launch traced here: 41.6 us
  Pallas kernels  41.5 us (100%)
    pallas_call x1, Pallas kernels, fused(): pl.pallas_call(functools.partial(sigma_kernel, geometry), out_shape=(pltp...  40.2 us
    pallas_call x1, Pallas kernels, fused(): pl.pallas_call(functools.partial(close_kernel, tile), out_shape=jax.Shape...  1.32 us

profile of v5, /device:TPU:4, one launch (start us, length us, event | category | flops | bytes accessed | tf_op | source)
XLA Modules:
  0.0 41.6 jit_solution(86054711056084576)
XLA Ops:
  0.0 40.2 %sigma_build.1 = (f32[256,1024]{1,0:T(8,128)S(1)}, bf16[2,256,256]{2,1,0:T(8,128)(2,1)S(1)}, bf16[2,1024,256]{2,1,0:T(8,128)(2,1)S(1)}) custom-call(s32[11,2,16]{2,1,0:T(2,128)} %bitcast.6, s32[2,16]{1,0:T(2,128)} %a_counts_hbm.1, s32[11,2,32]{2,1,0:T(2,128)} %bitcast.7, s32[2,32]{1,0:T(2,128)} %b_counts_hbm.1, bf16[256,1024]{1,0:T(8,128)(2,1)} %c_hbm.1, ...), custom_call_target="tpu_custom_call" | custom-call | tf_op jit(solution)/shard_map/sigma_build/pallas_call | solution.py:530
  40.2 1.3 %close_sigma.1 = f32[256,1024]{1,0:T(8,128)} custom-call(f32[256,1024]{1,0:T(8,128)S(1)} %get-tuple-element.8.part, bf16[2,256,256]{2,1,0:T(8,128)(2,1)S(1)} %get-tuple-element.9.last, bf16[2,1024,256]{2,1,0:T(8,128)(2,1)S(1)} %get-tuple-element.10.last_b), custom_call_target="tpu_custom_call" | custom-call | tf_op jit(solution)/shard_map/close_sigma/pallas_call | solution.py:547

commit v6 on v5

--- a/solution.py
+++ b/solution.py
@@ -280,8 +280,8 @@
             src_ref=straight.at[1, j], dst_ref=across.at[opposite, j], send_sem=straight_send.at[1, j], recv_sem=across_recv.at[opposite, j],
             device_id={"alpha": far * PAIR + 1 - x}, device_id_type=MESH)
 
-    lightened = (z == 1) & (c < CORES)
-    forwards = (z == 1) & (c >= CORES) & (c < 2 * CORES)
+    lightened = (z == 1) & (c == 0)
+    forwards = (z == 1) & (c == CORES)
     beside = jnp.where(c < CORES, c + CORES, jnp.where(c < 2 * CORES, c - CORES, c))
 
     def aside_copy():
@@ -313,17 +313,36 @@
                 diagonal_copy(j).start()
                 straight_copy(j).start()
             else:
-                turned = lightened & (j == 0)
-
-                @pl.when(turned)
+                ahead = (c < CORES) & (x == 0)
+                behind = (c < CORES) & (x == 1)
+                previous = jnp.maximum(j - 1, 0)
+                kept = (j > 1) | ((j == 1) & jnp.logical_not(lightened))
+
+                @pl.when(lightened & (j == 0))
                 def _():
                     aside_copy().start()
 
-                @pl.when(jnp.logical_not(turned & (x == 0)))
+                @pl.when(ahead)
+                def _():
+                    straight_copy(j).start()
+
+                    @pl.when(kept)
+                    def _():
+                        diagonal_copy(previous).start()
+
+                    @pl.when(j == nb - 1)
+                    def _():
+                        diagonal_copy(j).start()
+
+                @pl.when(jnp.logical_not(ahead))
                 def _():
                     diagonal_copy(j).start()
 
-                @pl.when(jnp.logical_not(turned & (x == 1)))
+                @pl.when(behind & kept)
+                def _():
+                    straight_copy(previous).start()
+
+                @pl.when(jnp.logical_not(ahead) & (jnp.logical_not(behind) | (j == nb - 1)))
                 def _():
                     straight_copy(j).start()
 
@@ -627,7 +646,7 @@
     operators, local_rows, list_slots, block_size = a_blocks.shape
     na, nb = lax.axis_size("alpha"), lax.axis_size("beta")
     geometry = (na, nb, operators, list_slots, block_size, local_rows // block_size, coeffs.shape[1] // block_size)
-    fits = scratch_bytes(geometry) < VMEM_LIMIT * 3 // 4
+    fits = scratch_bytes(geometry) < KERNEL_LIMIT * 3 // 4
     shaped = FROM_A == 1 and FROM_B == 2 and na % PAIR == 0 and na > 3 * PAIR and nb & (nb - 1) == 0 and nb >= 2 * CORES
     build = functools.partial(fused, geometry) if fits and shaped else plain
     return build(coeffs, a_blocks, a_list, a_count, b_blocks, b_list, b_count)

time: 41.7 us -> 41.4 us (level)
  the two profiles are of different devices: /device:TPU:4 before, /device:TPU:0 now
where the time goes in v6:
time: 41.4 us; the launch traced here: 40.8 us
  Pallas kernels  40.8 us (99%)
    pallas_call x1, Pallas kernels, fused(): pl.pallas_call(functools.partial(sigma_kernel, geometry), out_shape=(pltp...  39.5 us
    pallas_call x1, Pallas kernels, fused(): pl.pallas_call(functools.partial(close_kernel, tile), out_shape=jax.Shape...  1.32 us

profile of v6, /device:TPU:0, one launch (start us, length us, event | category | flops | bytes accessed | tf_op | source)
XLA Modules:
  0.0 40.8 jit_solution(16804287503553929679)
XLA Ops:
  0.0 39.5 %sigma_build.1 = (f32[256,1024]{1,0:T(8,128)S(1)}, bf16[2,256,256]{2,1,0:T(8,128)(2,1)S(1)}, bf16[2,1024,256]{2,1,0:T(8,128)(2,1)S(1)}) custom-call(s32[11,2,16]{2,1,0:T(2,128)} %bitcast.6, s32[2,16]{1,0:T(2,128)} %a_counts_hbm.1, s32[11,2,32]{2,1,0:T(2,128)} %bitcast.7, s32[2,32]{1,0:T(2,128)} %b_counts_hbm.1, bf16[256,1024]{1,0:T(8,128)(2,1)} %c_hbm.1, ...), custom_call_target="tpu_custom_call" | custom-call | tf_op jit(solution)/shard_map/sigma_build/pallas_call | solution.py:549
  39.5 1.3 %close_sigma.1 = f32[256,1024]{1,0:T(8,128)} custom-call(f32[256,1024]{1,0:T(8,128)S(1)} %get-tuple-element.8.part, bf16[2,256,256]{2,1,0:T(8,128)(2,1)S(1)} %get-tuple-element.9.last, bf16[2,1024,256]{2,1,0:T(8,128)(2,1)S(1)} %get-tuple-element.10.last_b), custom_call_target="tpu_custom_call" | custom-call | tf_op jit(solution)/shard_map/close_sigma/pallas_call | solution.py:566

commit v7 on v6

--- a/solution.py
+++ b/solution.py
@@ -10,8 +10,8 @@
 FROM_A = 1
 FROM_B = 2
 PAIR = 2
+CORES = 2
 LAG = 3
-CORES = 2
 VMEM_LIMIT = 60 * 1024 * 1024
 KERNEL_LIMIT = 40 * 1024 * 1024
 MESH = pl.DeviceIdType.MESH
@@ -19,7 +19,7 @@
 
 def sigma_kernel(geometry, a_lists_hbm, a_counts_hbm, b_lists_hbm, b_counts_hbm, c_hbm, a_hbm, b_hbm, out_ref, last_ref, last_b_ref, a_lists, a_counts, b_lists, b_counts, a_vec, b_vec, cbuf, abuf, bbuf, picks, column, across, chosen,
                  straight, tail, adense, bdense, acc, small, table_sem, local_sem, beta_send, beta_recv, column_recv, up_send, down_send, across_send, across_recv,
-                 straight_send, tail_recv, aside_send):
+                 straight_send, tail_recv):
     na, nb, ops, slots, blk, row_blocks, col_blocks = geometry
     levels = na // PAIR
     rows = row_blocks * blk
@@ -280,25 +280,6 @@
             src_ref=straight.at[1, j], dst_ref=across.at[opposite, j], send_sem=straight_send.at[1, j], recv_sem=across_recv.at[opposite, j],
             device_id={"alpha": far * PAIR + 1 - x}, device_id_type=MESH)
 
-    lightened = (z == 1) & (c == 0)
-    forwards = (z == 1) & (c == CORES)
-    beside = jnp.where(c < CORES, c + CORES, jnp.where(c < 2 * CORES, c - CORES, c))
-
-    def aside_copy():
-        return pltpu.make_async_remote_copy(
-            src_ref=straight.at[1 - x, 0], dst_ref=tail.at[0], send_sem=aside_send.at[0], recv_sem=tail_recv.at[0],
-            device_id={"beta": beside}, device_id_type=MESH)
-
-    def forward_crossing():
-        return pltpu.make_async_remote_copy(
-            src_ref=tail.at[0], dst_ref=across.at[levels - 1, 0], send_sem=aside_send.at[1], recv_sem=across_recv.at[levels - 1, 0],
-            device_id={"alpha": a - 1, "beta": beside}, device_id_type=MESH)
-
-    def forward_direct():
-        return pltpu.make_async_remote_copy(
-            src_ref=tail.at[0], dst_ref=tail.at[0], send_sem=aside_send.at[1], recv_sem=tail_recv.at[0],
-            device_id={"alpha": a - PAIR, "beta": beside}, device_id_type=MESH)
-
     def arrive(lev, j, below):
         pltpu.make_async_remote_copy(
             src_ref=column.at[lev, j], dst_ref=column.at[lev, j], send_sem=up_send.at[lev, j], recv_sem=column_recv.at[lev, j],
@@ -316,17 +297,12 @@
                 ahead = (c < CORES) & (x == 0)
                 behind = (c < CORES) & (x == 1)
                 previous = jnp.maximum(j - 1, 0)
-                kept = (j > 1) | ((j == 1) & jnp.logical_not(lightened))
-
-                @pl.when(lightened & (j == 0))
-                def _():
-                    aside_copy().start()
 
                 @pl.when(ahead)
                 def _():
                     straight_copy(j).start()
 
-                    @pl.when(kept)
+                    @pl.when(j > 0)
                     def _():
                         diagonal_copy(previous).start()
 
@@ -338,7 +314,7 @@
                 def _():
                     diagonal_copy(j).start()
 
-                @pl.when(behind & kept)
+                @pl.when(behind & (j > 0))
                 def _():
                     straight_copy(previous).start()
 
@@ -364,18 +340,6 @@
         j = i % nb
         distance = i // nb + 1
 
-        @pl.when((i == relayed - nb + 1) & forwards)
-        def _():
-            aside_copy().wait_recv()
-
-            @pl.when(x == 0)
-            def _():
-                forward_crossing().start()
-
-            @pl.when(x == 1)
-            def _():
-                forward_direct().start()
-
         @pl.when((i < relayed) & (z - distance >= 0))
         def _():
             arrive(z - distance, j, True)
@@ -403,7 +367,6 @@
             combine(z + distance_before, j_before)
 
         build_some(built + 2 * i, 2)
-
 
         early = i - (relayed + LAG - nb)
 
@@ -456,23 +419,8 @@
 
         @pl.when(up_last | down_last)
         def _():
-            turned = lightened & (j == 0)
-
-            @pl.when(turned)
-            def _():
-                aside_copy().wait_send()
-
-            @pl.when(jnp.logical_not(turned & (x == 1)))
-            def _():
-                straight_copy(j).wait_send()
-
-            @pl.when(jnp.logical_not(turned & (x == 0)))
-            def _():
-                diagonal_copy(j).wait_send()
-
-            @pl.when(forwards & (j == 0))
-            def _():
-                forward_direct().wait_send()
+            straight_copy(j).wait_send()
+            diagonal_copy(j).wait_send()
 
         @pl.when(jnp.logical_not(at_end & (lev == levels - 1 - z)))
         def _():
@@ -557,7 +505,7 @@
         ] + [pltpu.VMEM(shape, dtype) for shape, dtype in scratch_of(geometry, coeffs.dtype)] + [
             pltpu.SMEM((2 * levels + nb + PAIR,), jnp.int32),
             dma((6,)), dma((2 + col_blocks,)), dma((nb - 1,)), dma((nb - 1,)), dma((levels, nb)), dma((levels, nb)), dma((levels, nb)),
-            dma((levels, nb)), dma((levels, nb)), dma((PAIR, nb)), dma((nb,)), dma((2,)),
+            dma((levels, nb)), dma((levels, nb)), dma((PAIR, nb)), dma((nb,)),
         ],
         compiler_params=pltpu.CompilerParams(collective_id=0, has_side_effects=True, vmem_limit_bytes=KERNEL_LIMIT),
         name="sigma_build",
@@ -647,7 +595,7 @@
     na, nb = lax.axis_size("alpha"), lax.axis_size("beta")
     geometry = (na, nb, operators, list_slots, block_size, local_rows // block_size, coeffs.shape[1] // block_size)
     fits = scratch_bytes(geometry) < KERNEL_LIMIT * 3 // 4
-    shaped = FROM_A == 1 and FROM_B == 2 and na % PAIR == 0 and na > 3 * PAIR and nb & (nb - 1) == 0 and nb >= 2 * CORES
+    shaped = FROM_A == 1 and FROM_B == 2 and na % PAIR == 0 and na > 3 * PAIR and nb & (nb - 1) == 0 and nb > 1
     build = functools.partial(fused, geometry) if fits and shaped else plain
     return build(coeffs, a_blocks, a_list, a_count, b_blocks, b_list, b_count)
 

time: 41.4 us -> 41.8 us (level)
  the two profiles are of different devices: /device:TPU:0 before, /device:TPU:2 now
where the time goes in v7:
time: 41.8 us; the launch traced here: 41.6 us
  Pallas kernels  41.6 us (100%)
    pallas_call x1, Pallas kernels, fused(): pl.pallas_call(functools.partial(sigma_kernel, geometry), out_shape=(pltp...  40.3 us
    pallas_call x1, Pallas kernels, fused(): pl.pallas_call(functools.partial(close_kernel, tile), out_shape=jax.Shape...  1.32 us

profile of v7, /device:TPU:2, one launch (start us, length us, event | category | flops | bytes accessed | tf_op | source)
XLA Modules:
  0.0 41.6 jit_solution(12316650127419409257)
XLA Ops:
  0.0 40.3 %sigma_build.1 = (f32[256,1024]{1,0:T(8,128)S(1)}, bf16[2,256,256]{2,1,0:T(8,128)(2,1)S(1)}, bf16[2,1024,256]{2,1,0:T(8,128)(2,1)S(1)}) custom-call(s32[11,2,16]{2,1,0:T(2,128)} %bitcast.6, s32[2,16]{1,0:T(2,128)} %a_counts_hbm.1, s32[11,2,32]{2,1,0:T(2,128)} %bitcast.7, s32[2,32]{1,0:T(2,128)} %b_counts_hbm.1, bf16[256,1024]{1,0:T(8,128)(2,1)} %c_hbm.1, ...), custom_call_target="tpu_custom_call" | custom-call | tf_op jit(solution)/shard_map/sigma_build/pallas_call | solution.py:497
  40.3 1.3 %close_sigma.1 = f32[256,1024]{1,0:T(8,128)} custom-call(f32[256,1024]{1,0:T(8,128)S(1)} %get-tuple-element.8.part, bf16[2,256,256]{2,1,0:T(8,128)(2,1)S(1)} %get-tuple-element.9.last, bf16[2,1024,256]{2,1,0:T(8,128)(2,1)S(1)} %get-tuple-element.10.last_b), custom_call_target="tpu_custom_call" | custom-call | tf_op jit(solution)/shard_map/close_sigma/pallas_call | solution.py:514

commit v8 on v6

--- a/solution.py
+++ b/solution.py
@@ -10,7 +10,7 @@
 FROM_A = 1
 FROM_B = 2
 PAIR = 2
-LAG = 3
+LAG = 2
 CORES = 2
 VMEM_LIMIT = 60 * 1024 * 1024
 KERNEL_LIMIT = 40 * 1024 * 1024

time: 41.4 us -> 42.4 us (1.024); the launches traced: 40.8 us -> 42.3 us
  Pallas kernels: 40.8 us -> 42.3 us
    pallas_call x1, Pallas kernels: 39.5 us -> 41 us  [fused(): pl.pallas_call(functools.partial(sigma_kernel, geometry), out_shape=(pltp...]
where the time goes in v8:
time: 42.4 us; the launch traced here: 42.3 us
  Pallas kernels  42.3 us (100%)
    pallas_call x1, Pallas kernels, fused(): pl.pallas_call(functools.partial(sigma_kernel, geometry), out_shape=(pltp...  41 us
    pallas_call x1, Pallas kernels, fused(): pl.pallas_call(functools.partial(close_kernel, tile), out_shape=jax.Shape...  1.32 us

profile of v8, /device:TPU:0, one launch (start us, length us, event | category | flops | bytes accessed | tf_op | source)
XLA Modules:
  0.0 42.3 jit_solution(9740871602898236102)
XLA Ops:
  0.0 41.0 %sigma_build.1 = (f32[256,1024]{1,0:T(8,128)S(1)}, bf16[2,256,256]{2,1,0:T(8,128)(2,1)S(1)}, bf16[2,1024,256]{2,1,0:T(8,128)(2,1)S(1)}) custom-call(s32[11,2,16]{2,1,0:T(2,128)} %bitcast.6, s32[2,16]{1,0:T(2,128)} %a_counts_hbm.1, s32[11,2,32]{2,1,0:T(2,128)} %bitcast.7, s32[2,32]{1,0:T(2,128)} %b_counts_hbm.1, bf16[256,1024]{1,0:T(8,128)(2,1)} %c_hbm.1, ...), custom_call_target="tpu_custom_call" | custom-call | tf_op jit(solution)/shard_map/sigma_build/pallas_call | solution.py:549
  41.0 1.3 %close_sigma.1 = f32[256,1024]{1,0:T(8,128)} custom-call(f32[256,1024]{1,0:T(8,128)S(1)} %get-tuple-element.8.part, bf16[2,256,256]{2,1,0:T(8,128)(2,1)S(1)} %get-tuple-element.9.last, bf16[2,1024,256]{2,1,0:T(8,128)(2,1)S(1)} %get-tuple-element.10.last_b), custom_call_target="tpu_custom_call" | custom-call | tf_op jit(solution)/shard_map/close_sigma/pallas_call | solution.py:566
